TPU v7x, 256 devices: a whole 4x4x8 slice. The times are simulated.
256 devices in a mesh: pol: 2 (over y_lo), row: 4 (over x), col: 32 (over z, y_hi, core).
Axes of the slice: x: 4, y: 4 (y_hi: 2, y_lo: 2; y = y_hi * 2 + y_lo), z: 8, core: 2. Of those that a mesh axis runs over, the one named last changes fastest.
Arguments:
- kernel_half: bfloat16 [16384, 16384], P('row', ('pol', 'col')), may hold values from -0.046875 to 0.046875
- dipole: float32 [3, 16384], P(None, 'row'), may hold values from -6 to 6
- band_energy: float32 [8, 512], P('row'), may hold values from 0 to 4
- core_energy: float32 [4], replicated, may hold values from -2 to 2
- core_index: int32 [32], P('row'), may hold values from 0 to 3
Outputs:
- alphas: float32 [3, 2], replicated
- betas: float32 [3, 2], replicated
- last_vector: float32 [3, 16384], P(None, 'row')
All inputs are finite; a program needn't handle non-finite values.
Results may differ from a plain program's by a relative error of at most 0.0026.
Values may be sent and summed in bfloat16 or wider, within the bound.
A program may use at most 64 MiB of HBM per device.

v0:
```python
import jax
import jax.numpy as jnp
from jax import lax
from jax.sharding import PartitionSpec as P

CORES = 4
ITERS = 2


def copy_for_each(x, axis):
    count = lax.axis_size(axis)
    return lax.all_to_all(jnp.broadcast_to(x[None], (count, *x.shape)), axis, 0, 0, tiled=True)


def over_copies(x, axis):
    everything = copy_for_each(x, axis)
    return jnp.sum(everything, axis=0)


def in_order(blocks, dim):
    blocks = jnp.moveaxis(blocks, 0, dim)
    lengths = blocks.shape
    return blocks.reshape(*lengths[:dim], lengths[dim] * lengths[dim + 1], *lengths[dim + 2 :])


def gathered_copies(x, axis, dim):
    return in_order(copy_for_each(x, axis), dim)


def split_up(x, dim, count):
    before, after = (x.shape[:dim], x.shape[dim + 1 :])
    return jnp.moveaxis(x.reshape(*before, count, -1, *after), dim, 0)


def sum_at_owner(x, axis, dim):
    count = lax.axis_size(axis)
    blocks = lax.all_to_all(split_up(x, dim, count), axis, 0, 0, tiled=True)
    return jnp.sum(blocks, axis=0)


def padded_to(lines, count):
    spare = -len(lines) % count
    return jnp.pad(lines, [(0, spare)] + [(0, 0)] * (lines.ndim - 1))


def nested_sum(x, axes):
    lines = x.reshape(-1)
    own = sum_at_owner(padded_to(lines, lax.axis_size(axes)), axes, 0)
    whole = gathered_copies(own, axes, 0)
    return whole[: len(lines)].reshape(x.shape)


def packed_total(arrays, axis):
    line, at, done = (jnp.concatenate([a.reshape(-1) for a in arrays]), 0, [])
    running = over_copies(line, axis)
    for a in arrays:
        done.append(running[at : at + a.size].reshape(a.shape))
        at += a.size
    return tuple(done)


def local(kernel_half, dipole, band_energy, core_energy, core_index):
    row_count = kernel_half.shape[0]
    col_count = kernel_half.shape[1]
    col_start = (lax.axis_index("pol") * lax.axis_size("col") + lax.axis_index("col")) * col_count
    row_start = lax.axis_index("row") * row_count
    one_hot = (core_index[:, None] == jnp.arange(CORES, dtype=jnp.int32)[None, :]).astype(
        jnp.float32
    )
    offset = jnp.sum(one_hot * core_energy[None, :], axis=1)
    energy = (band_energy[:, None, :] - offset.reshape(-1, CORES)[:, :, None]).reshape(-1)
    start_sq = over_copies(jnp.sum(dipole * dipole, axis=1), "row")
    vector = dipole / jnp.sqrt(start_sq)[:, None]
    previous = jnp.zeros_like(vector)
    beta_now = jnp.zeros((dipole.shape[0],), jnp.float32)
    alpha_list = []
    beta_list = []
    for repeat in range(ITERS):
        local_bf = vector.astype(jnp.bfloat16)
        gathered = gathered_copies(local_bf, "row", 1)
        picked = lax.dynamic_slice_in_dim(gathered, col_start, col_count, 1)
        row_part = lax.dot_general(
            picked, kernel_half, (((1,), (1,)), ((), ())), preferred_element_type=jnp.float32
        )
        col_part = jnp.dot(local_bf, kernel_half, preferred_element_type=jnp.float32)
        row_sum = nested_sum(row_part, ("pol", "col"))
        col_sum = over_copies(col_part, "row")
        spread = gathered_copies(col_sum, ("pol", "col"), 1)
        coupled = row_sum + lax.dynamic_slice_in_dim(spread, row_start, row_count, 1)
        applied = energy[None, :] * vector + coupled
        products = packed_total(
            (
                jnp.sum(applied * applied, axis=1),
                jnp.sum(vector * applied, axis=1),
                jnp.sum(previous * applied, axis=1),
                jnp.sum(vector * vector, axis=1),
                jnp.sum(previous * previous, axis=1),
                jnp.sum(vector * previous, axis=1),
            ),
            "row",
        )
        alpha_now = products[1]
        squared = (
            products[0]
            - 2.0 * alpha_now * products[1]
            - 2.0 * beta_now * products[2]
            + alpha_now * alpha_now * products[3]
            + beta_now * beta_now * products[4]
            + 2.0 * alpha_now * beta_now * products[5]
        )
        leftover = applied - alpha_now[:, None] * vector - beta_now[:, None] * previous
        beta_next = jnp.sqrt(squared)
        previous = vector
        vector = leftover / beta_next[:, None]
        beta_now = beta_next
        alpha_list.append(alpha_now)
        beta_list.append(beta_next)
    return (jnp.stack(alpha_list, axis=1), jnp.stack(beta_list, axis=1), vector)


def solution(mesh):
    in_specs = (P("row", ("pol", "col")), P(None, "row"), P("row", None), P(), P("row"))
    out_specs = (P(), P(), P(None, "row"))
    return jax.shard_map(local, mesh=mesh, in_specs=in_specs, out_specs=out_specs, check_vma=False)
```

profile of v0, /device:TPU:1, one launch (start us, length us, event | category | flops | bytes accessed | tf_op | source)
XLA Modules:
  0.0 171.8 jit_solution(4596509342140488809)
XLA Ops:
  0.6 1.1 multiply_reduce_fusion.10
  1.8 8.8 %all_to_all.80 = f32[4,1,3]{2,1,0:T(1,128)S(1)} all-to-all(f32[4,1,3]{2,1,0:T(1,128)S(1)} %broadcast_in_dim.24), channel_id=1, replica_groups=mesh['pol'=2,'row'=4,'col'=32] {'row'}, dimensions={0} | all-to-all | bytes 96 | tf_op jit(solution)/shard_map/all_to_all | solution.py:12
  10.6 0.9 fusion.14
  11.5 0.7 broadcast_in_dim.25
  12.2 3.3 %all-to-all-start.1 = ((bf16[4,3,4096]{2,1,0:T(4,128)(2,1)}), bf16[4,3,4096]{2,1,0:T(4,128)(2,1)S(1)}, u32[]{:S(2)}, u32[]{:S(2)}) async-start(bf16[4,3,4096]{2,1,0:T(4,128)(2,1)} %broadcast_in_dim.25), calls=%async_computation.1 | async-start | bytes 262144 | tf_op jit(solution)/shard_map/all_to_all | solution.py:12
  15.5 4.8 %all-to-all-done.1 = bf16[4,3,4096]{2,1,0:T(4,128)(2,1)S(1)} async-done(((bf16[4,3,4096]{2,1,0:T(4,128)(2,1)}), bf16[4,3,4096]{2,1,0:T(4,128)(2,1)S(1)}, u32[]{:S(2)}, u32[]{:S(2)}) %all-to-all-start.1) | async-done | bytes 98336 | tf_op jit(solution)/shard_map/all_to_all | solution.py:12
  20.3 0.6 fusion.2
  21.0 0.8 all_to_all.65
  21.8 14.9 %all-to-all-start.2 = ((f32[64,1,192]{2,1,0:T(1,128)}), f32[64,1,192]{2,1,0:T(1,128)S(1)}, u32[]{:S(2)}, u32[]{:S(2)}) async-start(f32[64,1,192]{2,1,0:T(1,128)} %all_to_all.65), calls=%async_computation.2 | async-start | bytes 131072 | tf_op jit(solution)/shard_map/all_to_all | solution.py:37
  36.7 0.4 fusion.16
  37.1 9.3 %all-to-all-done.2 = f32[64,1,192]{2,1,0:T(1,128)S(1)} async-done(((f32[64,1,192]{2,1,0:T(1,128)}), f32[64,1,192]{2,1,0:T(1,128)S(1)}, u32[]{:S(2)}, u32[]{:S(2)}) %all-to-all-start.2) | async-done | bytes 49184 | tf_op jit(solution)/shard_map/all_to_all | solution.py:37
  46.4 0.6 broadcast_in_dim.27
  47.0 3.3 %all-to-all-start.4 = ((f32[4,3,256]{2,1,0:T(4,128)}), f32[4,3,256]{2,1,0:T(4,128)S(1)}, u32[]{:S(2)}, u32[]{:S(2)}) async-start(f32[4,3,256]{2,1,0:T(4,128)} %broadcast_in_dim.27), calls=%async_computation.4 | async-start | bytes 32768 | tf_op jit(solution)/shard_map/all_to_all | solution.py:12
  50.2 0.1 reduce_sum.184
  50.3 4.1 %all-to-all-done.4 = f32[4,3,256]{2,1,0:T(4,128)S(1)} async-done(((f32[4,3,256]{2,1,0:T(4,128)}), f32[4,3,256]{2,1,0:T(4,128)S(1)}, u32[]{:S(2)}, u32[]{:S(2)}) %all-to-all-start.4) | async-done | bytes 12320 | tf_op jit(solution)/shard_map/all_to_all | solution.py:12
  54.4 0.7 broadcast_in_dim.26
  55.1 5.6 %all-to-all-start.3 = ((f32[64,1,192]{2,1,0:T(1,128)}), f32[64,1,192]{2,1,0:T(1,128)S(1)}, u32[]{:S(2)}, u32[]{:S(2)}) async-start(f32[64,1,192]{2,1,0:T(1,128)} %broadcast_in_dim.26), calls=%async_computation.3 | async-start | bytes 131072 | tf_op jit(solution)/shard_map/all_to_all | solution.py:12
  60.7 9.8 %all-to-all-done.3 = f32[64,1,192]{2,1,0:T(1,128)S(1)} async-done(((f32[64,1,192]{2,1,0:T(1,128)}), f32[64,1,192]{2,1,0:T(1,128)S(1)}, u32[]{:S(2)}, u32[]{:S(2)}) %all-to-all-start.3) | async-done | bytes 49184 | tf_op jit(solution)/shard_map/all_to_all | solution.py:12
  70.5 0.7 broadcast_in_dim.28
  71.2 4.4 %all-to-all-start.5 = ((f32[64,3,256]{2,1,0:T(4,128)}), f32[64,3,256]{2,1,0:T(4,128)S(1)}, u32[]{:S(2)}, u32[]{:S(2)}) async-start(f32[64,3,256]{2,1,0:T(4,128)} %broadcast_in_dim.28), calls=%async_computation.5 | async-start | bytes 524288 | tf_op jit(solution)/shard_map/all_to_all | solution.py:12
  75.9 0.2 reduce.5
  76.1 0.1 reshape_reshape.6
  76.2 12.4 %all-to-all-done.5 = f32[64,3,256]{2,1,0:T(4,128)S(1)} async-done(((f32[64,3,256]{2,1,0:T(4,128)}), f32[64,3,256]{2,1,0:T(4,128)S(1)}, u32[]{:S(2)}, u32[]{:S(2)}) %all-to-all-start.5) | async-done | bytes 196640 | tf_op jit(solution)/shard_map/all_to_all | solution.py:12
  88.6 0.2 multiply_reduce_fusion.5
  88.9 6.5 %all_to_all.81 = f32[4,1,18]{2,1,0:T(1,128)S(1)} all-to-all(f32[4,1,18]{2,1,0:T(1,128)S(1)} %broadcast_in_dim.29), channel_id=1, replica_groups=mesh['pol'=2,'row'=4,'col'=32] {'row'}, dimensions={0} | all-to-all | bytes 576 | tf_op jit(solution)/shard_map/all_to_all | solution.py:12
  95.5 0.1 fusion.13
  95.6 7.2 %all_to_all.82 = bf16[4,3,4096]{2,1,0:T(4,128)(2,1)S(1)} all-to-all(bf16[4,3,4096]{2,1,0:T(4,128)(2,1)S(1)} %broadcast_in_dim.30), channel_id=1, replica_groups=mesh['pol'=2,'row'=4,'col'=32] {'row'}, dimensions={0} | all-to-all | bytes 196608 | tf_op jit(solution)/shard_map/all_to_all | solution.py:12
  102.8 0.6 fusion
  103.5 0.8 all_to_all.66
  104.3 7.5 %all-to-all-start.8 = ((f32[64,1,192]{2,1,0:T(1,128)}), f32[64,1,192]{2,1,0:T(1,128)S(1)}, u32[]{:S(2)}, u32[]{:S(2)}) async-start(f32[64,1,192]{2,1,0:T(1,128)} %all_to_all.66), calls=%async_computation.8 | async-start | bytes 131072 | tf_op jit(solution)/shard_map/all_to_all | solution.py:37
  111.7 0.4 fusion.17
  112.1 9.3 %all-to-all-done.8 = f32[64,1,192]{2,1,0:T(1,128)S(1)} async-done(((f32[64,1,192]{2,1,0:T(1,128)}), f32[64,1,192]{2,1,0:T(1,128)S(1)}, u32[]{:S(2)}, u32[]{:S(2)}) %all-to-all-start.8) | async-done | bytes 49184 | tf_op jit(solution)/shard_map/all_to_all | solution.py:37
  121.4 0.6 broadcast_in_dim.32
  122.0 3.3 %all-to-all-start.10 = ((f32[4,3,256]{2,1,0:T(4,128)}), f32[4,3,256]{2,1,0:T(4,128)S(1)}, u32[]{:S(2)}, u32[]{:S(2)}) async-start(f32[4,3,256]{2,1,0:T(4,128)} %broadcast_in_dim.32), calls=%async_computation.10 | async-start | bytes 32768 | tf_op jit(solution)/shard_map/all_to_all | solution.py:12
  125.3 0.1 reduce_sum.193
  125.4 4.1 %all-to-all-done.10 = f32[4,3,256]{2,1,0:T(4,128)S(1)} async-done(((f32[4,3,256]{2,1,0:T(4,128)}), f32[4,3,256]{2,1,0:T(4,128)S(1)}, u32[]{:S(2)}, u32[]{:S(2)}) %all-to-all-start.10) | async-done | bytes 12320 | tf_op jit(solution)/shard_map/all_to_all | solution.py:12
  129.5 0.7 broadcast_in_dim.31
  130.1 5.6 %all-to-all-start.9 = ((f32[64,1,192]{2,1,0:T(1,128)}), f32[64,1,192]{2,1,0:T(1,128)S(1)}, u32[]{:S(2)}, u32[]{:S(2)}) async-start(f32[64,1,192]{2,1,0:T(1,128)} %broadcast_in_dim.31), calls=%async_computation.9 | async-start | bytes 131072 | tf_op jit(solution)/shard_map/all_to_all | solution.py:12
  135.7 9.8 %all-to-all-done.9 = f32[64,1,192]{2,1,0:T(1,128)S(1)} async-done(((f32[64,1,192]{2,1,0:T(1,128)}), f32[64,1,192]{2,1,0:T(1,128)S(1)}, u32[]{:S(2)}, u32[]{:S(2)}) %all-to-all-start.9) | async-done | bytes 49184 | tf_op jit(solution)/shard_map/all_to_all | solution.py:12
  145.5 0.7 broadcast_in_dim.33
  146.2 4.4 %all-to-all-start.11 = ((f32[64,3,256]{2,1,0:T(4,128)}), f32[64,3,256]{2,1,0:T(4,128)S(1)}, u32[]{:S(2)}, u32[]{:S(2)}) async-start(f32[64,3,256]{2,1,0:T(4,128)} %broadcast_in_dim.33), calls=%async_computation.11 | async-start | bytes 524288 | tf_op jit(solution)/shard_map/all_to_all | solution.py:12
  150.7 0.2 reduce.6
  150.9 0.1 reshape_reshape.7
  151.0 12.7 %all-to-all-done.11 = f32[64,3,256]{2,1,0:T(4,128)S(1)} async-done(((f32[64,3,256]{2,1,0:T(4,128)}), f32[64,3,256]{2,1,0:T(4,128)S(1)}, u32[]{:S(2)}, u32[]{:S(2)}) %all-to-all-start.11) | async-done | bytes 196640 | tf_op jit(solution)/shard_map/all_to_all | solution.py:12
  163.6 0.2 multiply_reduce_fusion
  163.9 6.5 %all_to_all.83 = f32[4,1,18]{2,1,0:T(1,128)S(1)} all-to-all(f32[4,1,18]{2,1,0:T(1,128)S(1)} %broadcast_in_dim.34), channel_id=1, replica_groups=mesh['pol'=2,'row'=4,'col'=32] {'row'}, dimensions={0} | all-to-all | bytes 576 | tf_op jit(solution)/shard_map/all_to_all | solution.py:12
  170.5 0.7 subtract_divide_fusion
  171.2 0.6 pad_maximum_fusion
  (27 shorter events, 0.8 us)
Async XLA Ops:
  0.6 19.7 %copy-start = (bf16[4096,256]{1,0:T(8,128)(2,1)S(1)}, bf16[4096,256]{1,0:T(8,128)(2,1)}, u32[]{:S(2)}) copy-start(bf16[4096,256]{1,0:T(8,128)(2,1)} %param.5) | copy-start | bytes 6291460
  12.2 8.1 %all-to-all-start.1 = ((bf16[4,3,4096]{2,1,0:T(4,128)(2,1)}), bf16[4,3,4096]{2,1,0:T(4,128)(2,1)S(1)}, u32[]{:S(2)}, u32[]{:S(2)}) async-start(bf16[4,3,4096]{2,1,0:T(4,128)(2,1)} %broadcast_in_dim.25), calls=%async_computation.1 | async-start | bytes 262144 | tf_op jit(solution)/shard_map/all_to_all | solution.py:12
  21.0 54.7 %copy-start.2 = (f32[4]{0:T(128)S(1)}, f32[4]{0:T(128)}, u32[]{:S(2)}) copy-start(f32[4]{0:T(128)} %param.8) | copy-start | bytes 52
  21.0 54.7 %copy-start.3 = (s32[8]{0:T(128)S(1)}, s32[8]{0:T(128)}, u32[]{:S(2)}) copy-start(s32[8]{0:T(128)} %param.9) | copy-start | bytes 100
  21.0 54.9 %copy-start.1 = (f32[2,512]{1,0:T(2,128)S(1)}, f32[2,512]{1,0:T(2,128)}, u32[]{:S(2)}) copy-start(f32[2,512]{1,0:T(2,128)} %param.7) | copy-start | bytes 12292
  21.8 24.6 %all-to-all-start.2 = ((f32[64,1,192]{2,1,0:T(1,128)}), f32[64,1,192]{2,1,0:T(1,128)S(1)}, u32[]{:S(2)}, u32[]{:S(2)}) async-start(f32[64,1,192]{2,1,0:T(1,128)} %all_to_all.65), calls=%async_computation.2 | async-start | bytes 131072 | tf_op jit(solution)/shard_map/all_to_all | solution.py:37
  47.0 7.4 %all-to-all-start.4 = ((f32[4,3,256]{2,1,0:T(4,128)}), f32[4,3,256]{2,1,0:T(4,128)S(1)}, u32[]{:S(2)}, u32[]{:S(2)}) async-start(f32[4,3,256]{2,1,0:T(4,128)} %broadcast_in_dim.27), calls=%async_computation.4 | async-start | bytes 32768 | tf_op jit(solution)/shard_map/all_to_all | solution.py:12
  55.1 15.4 %all-to-all-start.3 = ((f32[64,1,192]{2,1,0:T(1,128)}), f32[64,1,192]{2,1,0:T(1,128)S(1)}, u32[]{:S(2)}, u32[]{:S(2)}) async-start(f32[64,1,192]{2,1,0:T(1,128)} %broadcast_in_dim.26), calls=%async_computation.3 | async-start | bytes 131072 | tf_op jit(solution)/shard_map/all_to_all | solution.py:12
  71.2 17.4 %all-to-all-start.5 = ((f32[64,3,256]{2,1,0:T(4,128)}), f32[64,3,256]{2,1,0:T(4,128)S(1)}, u32[]{:S(2)}, u32[]{:S(2)}) async-start(f32[64,3,256]{2,1,0:T(4,128)} %broadcast_in_dim.28), calls=%async_computation.5 | async-start | bytes 524288 | tf_op jit(solution)/shard_map/all_to_all | solution.py:12
  104.3 17.1 %all-to-all-start.8 = ((f32[64,1,192]{2,1,0:T(1,128)}), f32[64,1,192]{2,1,0:T(1,128)S(1)}, u32[]{:S(2)}, u32[]{:S(2)}) async-start(f32[64,1,192]{2,1,0:T(1,128)} %all_to_all.66), calls=%async_computation.8 | async-start | bytes 131072 | tf_op jit(solution)/shard_map/all_to_all | solution.py:37
  122.0 7.4 %all-to-all-start.10 = ((f32[4,3,256]{2,1,0:T(4,128)}), f32[4,3,256]{2,1,0:T(4,128)S(1)}, u32[]{:S(2)}, u32[]{:S(2)}) async-start(f32[4,3,256]{2,1,0:T(4,128)} %broadcast_in_dim.32), calls=%async_computation.10 | async-start | bytes 32768 | tf_op jit(solution)/shard_map/all_to_all | solution.py:12
  130.1 15.4 %all-to-all-start.9 = ((f32[64,1,192]{2,1,0:T(1,128)}), f32[64,1,192]{2,1,0:T(1,128)S(1)}, u32[]{:S(2)}, u32[]{:S(2)}) async-start(f32[64,1,192]{2,1,0:T(1,128)} %broadcast_in_dim.31), calls=%async_computation.9 | async-start | bytes 131072 | tf_op jit(solution)/shard_map/all_to_all | solution.py:12
  146.2 17.4 %all-to-all-start.11 = ((f32[64,3,256]{2,1,0:T(4,128)}), f32[64,3,256]{2,1,0:T(4,128)S(1)}, u32[]{:S(2)}, u32[]{:S(2)}) async-start(f32[64,3,256]{2,1,0:T(4,128)} %broadcast_in_dim.33), calls=%async_computation.11 | async-start | bytes 524288 | tf_op jit(solution)/shard_map/all_to_all | solution.py:12
where the time goes:
time: 173 us; the launch traced here: 172 us
  waiting for transfers between devices  76.1 us (44%)
  starting transfers between devices  52.3 us (30%)
  blocking collectives  28.9 us (17%)
  local copies, waits for them, and re-layouts  6.83 us (4%)
  other arithmetic  4.85 us (3%)
  matrix products  2.03 us (1%)
    all_to_all x7, waiting for transfers between devices, copy_for_each(): lax.all_to_all(jnp.broadcast_to(x[None], (count, *x.shape)), axis, 0, 0,...  57.5 us
    all_to_all x7, starting transfers between devices, copy_for_each(): lax.all_to_all(jnp.broadcast_to(x[None], (count, *x.shape)), axis, 0, 0,...  29.9 us
    all_to_all x4, blocking collectives, copy_for_each(): lax.all_to_all(jnp.broadcast_to(x[None], (count, *x.shape)), axis, 0, 0,...  28.9 us
    all_to_all x2, starting transfers between devices, sum_at_owner(): blocks = lax.all_to_all(split_up(x, dim, count), axis, 0, 0, tiled=True)  22.4 us
    all_to_all x2, waiting for transfers between devices, sum_at_owner(): blocks = lax.all_to_all(split_up(x, dim, count), axis, 0, 0, tiled=True)  18.6 us
    broadcast_in_dim x11, local copies, waits for them, and re-layouts, copy_for_each(): jnp.broadcast_to(x[None], (count, *x.shape))  4.73 us
  transfers between devices with their start and end apart: 9, of which 9 were waited for; matrix products, arithmetic and copies ran while one was open for 1% of the time, Pallas kernels for 0%

commit v1 on v0

v1 whole, which is shorter than its diff:
```python
import functools

import jax
import jax.numpy as jnp
from jax import lax
from jax.experimental import pallas as pl
from jax.experimental.pallas import tpu as pltpu
from jax.sharding import PartitionSpec as P

F32 = jnp.float32
BF = jnp.bfloat16
MESH = pl.DeviceIdType.MESH
CORES = 4
LANES = 128
ROWS = 16
QUARTERS = 4
POLS = 3


def iota(width, dim=0):
    return lax.broadcasted_iota(jnp.int32, (ROWS, width), dim)


def spread(parts):
    width = parts[0].shape[1]
    row = iota(width)
    a, b, c = (jnp.broadcast_to(t, (ROWS, width)) for t in parts)
    return jnp.where(row < 4, a, jnp.where(row < 8, b, jnp.where(row < 12, c, 0.0)))


def over_quarters(x):
    return [jnp.sum(x[4 * q : 4 * q + 4], axis=0, keepdims=True) for q in range(POLS)]


def placed(parts, first, rows):
    row = lax.broadcasted_iota(jnp.int32, (rows, LANES), 0)
    out = jnp.zeros((rows, LANES), F32)
    for q in range(POLS):
        out = jnp.where(row == first + q, jnp.broadcast_to(parts[q], (rows, LANES)), out)
    return out


def halves(x):
    high = x.astype(BF)
    return jnp.concatenate([high, (x - high.astype(F32)).astype(BF)], axis=0)


def joined(x):
    return x[:ROWS] + x[ROWS:]


def kernel(
    sizes,
    w_hbm, dip_hbm, band_hbm, core_hbm, index_hbm,
    alpha_ref, beta_ref, last_ref,
    w, dip, band, core, index,
    uc0, u, en, ub,
    send1, recv1, sendc, recvc, send2, recv2, send3, recv3, recvt, sendx, recvx,
    load_sem, core_sem, s0, r0, s1, r1, sc, rc, s2, r2, s3, r3, st, rt, sx, rx,
):
    nx, nz, zl_count = sizes
    zh_count = nz // zl_count
    p = lax.axis_index("pol")
    x = lax.axis_index("row")
    col = lax.axis_index("col")
    z = col // 4
    h = (col // 2) % 2
    k = col % 2
    g_me = h * 4 + k * 2 + p
    zl = z % zl_count
    home = p * zh_count + z // zl_count
    is_home = x == home
    keeper = (z // zl_count) == (x % zh_count)
    p_keep = x // zh_count

    def dev(pp, xx, zz, hh, kk):
        return (pp, xx, zz * 4 + hh * 2 + kk)

    loads = [
        pltpu.make_async_copy(dip_hbm, dip, load_sem.at[0]),
        pltpu.make_async_copy(band_hbm, band, load_sem.at[1]),
        pltpu.make_async_copy(core_hbm, core, core_sem.at[0]),
        pltpu.make_async_copy(index_hbm, index, core_sem.at[1]),
    ]
    for c in loads:
        c.start()
    big = w.shape[0] // 4
    w_loads = [
        pltpu.make_async_copy(
            w_hbm.at[pl.ds(i * big, big)], w.at[pl.ds(i * big, big)], load_sem.at[2 + i]
        )
        for i in range(4)
    ]
    for c in w_loads:
        c.start()

    barrier = pltpu.get_barrier_semaphore()
    greeted = []
    for d in range(1, nz):
        greeted.append(dev(p, x, (z + d) % nz, h, k))
    for dx in range(1, nx):
        for dp in range(2):
            greeted.append(dev((p + dp) % 2, (x + dx) % nx, z, h, k))
    for j in range(1, 8):
        greeted.append(dev((p + j % 2) % 2, x, z, (h + j // 4) % 2, (k + (j // 2) % 2) % 2))
    for d in greeted:
        pl.semaphore_signal(barrier, inc=1, device_id=d, device_id_type=MESH)

    row = iota(LANES)
    row2 = iota(2 * LANES)
    ends = []

    def start(make, condition=None):
        ends.append((make, condition))
        if condition is None:
            make().start()
        else:
            pl.when(condition)(lambda: make().start())

    def finish():
        for make, condition in ends:
            if condition is None:
                make().wait_send()
            else:
                pl.when(condition)(lambda make=make: make().wait_send())


    for c in loads:
        c.wait()
    for g in range(8):
        u[0, g] = jnp.zeros((ROWS, LANES), F32)
        for q in range(POLS):
            for t in range(QUARTERS):
                at = (t * 8 + g) * LANES
                u[0, g, 4 * q + t : 4 * q + t + 1, :] = dip[q : q + 1, at : at + LANES]
    offsets = []
    for i in range(2 * CORES):
        level = index[i]
        off = jnp.float32(0.0)
        for j in range(CORES):
            off = jnp.where(level == j, core[j], off)
        offsets.append(off)
    for g in range(8):
        at = (g % 4) * LANES
        low = jnp.broadcast_to(band[0:1, at : at + LANES], (ROWS, LANES))
        high = jnp.broadcast_to(band[1:2, at : at + LANES], (ROWS, LANES))
        value = jnp.zeros((ROWS, LANES), F32)
        for t in range(QUARTERS):
            level = (low if t < 2 else high) - offsets[(t // 2) * 4 + (t % 2) * 2 + g // 4]
            value = jnp.where(row % 4 == t, level, value)
        en[g] = value

    pl.semaphore_wait(barrier, len(greeted))

    own_at = pl.multiple_of((zl * 4 + h * 2 + k) * 2 * LANES, 2 * LANES)

    def first_copy(dx):
        return pltpu.make_async_remote_copy(
            src_ref=dip.at[:, pl.ds(own_at, 2 * LANES)],
            dst_ref=uc0,
            send_sem=s0.at[dx - 1],
            recv_sem=r0.at[0],
            device_id=dev(p, (x + dx) % nx, z, h, k),
            device_id_type=MESH,
        )

    for dx in range(1, nx):
        start(functools.partial(first_copy, dx), is_home)

    @pl.when(is_home)
    def _():
        uc0[...] = dip[:, pl.ds(own_at, 2 * LANES)]

    for c in w_loads:
        c.wait()

    def tiles_of(hh, kk, t):
        return pl.ds(pl.multiple_of((t * 4 + hh * 2 + kk) * 2 * LANES, 2 * LANES), 2 * LANES)

    coefficients = []
    column = None
    for step in range(2):
        for g in range(8):
            ub[:, g * LANES : (g + 1) * LANES] = halves(u[step, g])
        block = 8 * LANES
        sums = jnp.zeros((ROWS, 2 * LANES), F32)
        for t in range(QUARTERS):
            part = joined(jnp.dot(ub[...], w[t * block : (t + 1) * block, :], preferred_element_type=F32))
            sums = jnp.where(row2 % 4 == t, part, sums)
        col_part = over_quarters(sums)
        col_rows = jnp.where(row2 % 4 == zl, spread(col_part), 0.0)
        for half in range(2):
            sendc[step, half] = col_rows[:, half * LANES : (half + 1) * LANES]

        def col_copy(half, step=step):
            return pltpu.make_async_remote_copy(
                src_ref=sendc.at[step, half],
                dst_ref=recvc.at[step, x],
                send_sem=sc.at[step, half],
                recv_sem=rc.at[step, x],
                device_id=dev(half, home, z, h, k),
                device_id_type=MESH,
            )

        for half in range(2):
            mine = jnp.logical_and(is_home, p == half)

            @pl.when(mine)
            def _(half=half, step=step):
                recvc[step, x] = sendc[step, half]

            start(functools.partial(col_copy, half), jnp.logical_not(mine))

        squares = jnp.zeros((ROWS, LANES), F32)
        weighted = jnp.zeros((ROWS, LANES), F32)
        for g in range(8):
            sq = u[step, g] * u[step, g]
            squares += sq
            weighted += en[g] * sq
        own_sums = placed(over_quarters(squares), 0, 8) + placed(over_quarters(weighted), 4, 8)

        if step == 0:

            @pl.when(jnp.logical_not(is_home))
            def _():
                first_copy(1).wait_recv()

            column = [uc0[q : q + 1, :] for q in range(POLS)]
        else:
            @pl.when(jnp.logical_not(is_home))
            def _():
                for half in range(2):
                    tile_copy(1, half).wait_recv()

            @pl.when(is_home)
            def _():
                for half in range(2):
                    recvt[half] = recv3[0, h * 4 + k * 2 + half]

            both = jnp.concatenate([recvt[0], recvt[1]], axis=1)
            arrived = over_quarters(jnp.where(row2 % 4 == zl, both, 0.0))
            alpha = coefficients[0][0]
            column = [arrived[q] - alpha[q][:, :1] * column[q] for q in range(POLS)]
        twice = []
        for q in range(POLS):
            line = 2.0 * col_part[q] * column[q]
            twice.append(line[:, :LANES] + line[:, LANES:])
        sum_rows = placed(twice, 12, ROWS)
        left = halves(spread(column))

        def row_copy(j, pp, step=step):
            jh, jk = 1 - j // 2, 1 - j % 2
            return pltpu.make_async_remote_copy(
                src_ref=send1.at[step, j, pp],
                dst_ref=recv1.at[step, g_me],
                send_sem=s1.at[step, j, pp],
                recv_sem=r1.at[step, g_me],
                device_id=dev(pp, x, z, (h + jh) % 2, (k + jk) % 2),
                device_id_type=MESH,
            )

        for j in range(4):
            jh, jk = 1 - j // 2, 1 - j % 2
            hh, kk = (h + jh) % 2, (k + jk) % 2
            lines = jnp.zeros((ROWS, 2 * LANES), F32)
            for t in range(QUARTERS):
                part = joined(lax.dot_general(
                    left, w[tiles_of(hh, kk, t), :], (((1,), (1,)), ((), ())),
                    preferred_element_type=F32,
                ))
                lines = jnp.where(row2 % 4 == t, part, lines)
            for pp in range(2):
                send1[step, j, pp] = lines[:, pp * LANES : (pp + 1) * LANES] + sum_rows
            if j < 3:
                for pp in range(2):
                    start(functools.partial(row_copy, j, pp))
            else:
                start(functools.partial(row_copy, j, 1 - p))
                recv1[step, g_me] = send1[step, j, p]

        for j in range(1, 8):
            g = (h + j // 4) % 2 * 4 + (k + (j // 2) % 2) % 2 * 2 + (p + j % 2) % 2
            pltpu.make_async_remote_copy(
                src_ref=send1.at[step, 0, 0], dst_ref=recv1.at[step, g], send_sem=s1.at[step, 0, 0],
                recv_sem=r1.at[step, g], device_id=dev(p, x, z, h, k), device_id_type=MESH,
            ).wait_recv()
        total = recv1[step, 0]
        for g in range(1, 8):
            total += recv1[step, g]
        send2[step] = total

        @pl.when(keeper)
        def _(step=step):
            for xx in range(nx):
                @pl.when(jnp.logical_not(jnp.logical_and(x == xx, p == p_keep)))
                def _(xx=xx):
                    pltpu.make_async_remote_copy(
                        src_ref=sendc.at[step, 0], dst_ref=recvc.at[step, xx], send_sem=sc.at[step, 0],
                        recv_sem=rc.at[step, xx], device_id=dev(p, x, z, h, k), device_id_type=MESH,
                    ).wait_recv()
            cols = recvc[step, 0]
            for xx in range(1, nx):
                cols += recvc[step, xx]
            send2[step] = send2[step] + cols

        def z_copy(d, step=step):
            return pltpu.make_async_remote_copy(
                src_ref=send2.at[step], dst_ref=recv2.at[step, z], send_sem=s2.at[step, d - 1],
                recv_sem=r2.at[step, z], device_id=dev(p, x, (z + d) % nz, h, k), device_id_type=MESH,
            )

        for d in sorted(range(1, nz), key=lambda d: -min(d, nz - d)):
            start(functools.partial(z_copy, d))
        recv2[step, z] = send2[step]
        for d in range(1, nz):
            zz = (z + d) % nz
            pltpu.make_async_remote_copy(
                src_ref=send2.at[step], dst_ref=recv2.at[step, zz], send_sem=s2.at[step, d - 1],
                recv_sem=r2.at[step, zz], device_id=dev(p, x, z, h, k), device_id_type=MESH,
            ).wait_recv()
        total = recv2[step, 0]
        for zz in range(1, nz):
            total += recv2[step, zz]

        low = lax.broadcasted_iota(jnp.int32, (8, LANES), 0)
        sendx[step] = jnp.where(low >= 4, total[8:], 0.0) + own_sums

        def x_copy(dx, at):
            return pltpu.make_async_remote_copy(
                src_ref=sendx.at[at], dst_ref=recvx.at[at, x], send_sem=sx.at[at, dx - 1],
                recv_sem=rx.at[at, x], device_id=dev(p, (x + dx) % nx, z, h, k), device_id_type=MESH,
            )

        def x_wait(dx, at):
            xx = (x + dx) % nx
            pltpu.make_async_remote_copy(
                src_ref=sendx.at[at], dst_ref=recvx.at[at, xx], send_sem=sx.at[at, dx - 1],
                recv_sem=rx.at[at, xx], device_id=dev(p, x, z, h, k), device_id_type=MESH,
            ).wait_recv()

        for dx in range(1, nx):
            start(functools.partial(x_copy, dx, step))
        recvx[step, x] = sendx[step]
        send3[step] = total + en[g_me] * u[step, g_me]

        def tile_copy(dx, half):
            return pltpu.make_async_remote_copy(
                src_ref=send3.at[0], dst_ref=recvt.at[half], send_sem=st.at[dx - 1],
                recv_sem=rt.at[half], device_id=dev(p_keep, (x + dx) % nx, z, h, k), device_id_type=MESH,
            )

        if step == 0:
            for dx in range(1, nx):
                start(functools.partial(tile_copy, dx, p), keeper)

        def chunk_copy(j, step=step):
            return pltpu.make_async_remote_copy(
                src_ref=send3.at[step], dst_ref=recv3.at[step, g_me], send_sem=s3.at[step, j - 1],
                recv_sem=r3.at[step, g_me],
                device_id=dev((p + j % 2) % 2, x, z, (h + j // 4) % 2, (k + (j // 2) % 2) % 2),
                device_id_type=MESH,
            )

        for j in range(7, 0, -1):
            start(functools.partial(chunk_copy, j))
        recv3[step, g_me] = send3[step]

        for dx in range(1, nx):
            x_wait(dx, step)
        sums = recvx[step, 0]
        for xx in range(1, nx):
            sums += recvx[step, xx]
        sums = jnp.broadcast_to(jnp.sum(sums, axis=1, keepdims=True), (8, LANES))
        norms = [sums[q : q + 1] for q in range(POLS)]
        alpha = [sums[4 + q : 5 + q] / norms[q] for q in range(POLS)]
        coefficients.append((alpha, norms))

        for j in range(1, 8):
            g = (h + j // 4) % 2 * 4 + (k + (j // 2) % 2) % 2 * 2 + (p + j % 2) % 2
            pltpu.make_async_remote_copy(
                src_ref=send3.at[step], dst_ref=recv3.at[step, g], send_sem=s3.at[step, j - 1],
                recv_sem=r3.at[step, g], device_id=dev(p, x, z, h, k), device_id_type=MESH,
            ).wait_recv()
        factor = spread(alpha)
        if step == 0:
            for g in range(8):
                u[1, g] = recv3[0, g] - factor * u[0, g]

    (alpha0, norm0), (alpha1, norm1) = coefficients
    ratio = [norm1[q] / norm0[q] for q in range(POLS)]
    back = spread(ratio)
    squares = jnp.zeros((ROWS, LANES), F32)
    last = []
    for g in range(8):
        value = recv3[1, g] - factor * u[1, g] - back * u[0, g]
        squares += value * value
        last.append(value)
    sendx[2] = placed(over_quarters(squares), 0, 8)
    for dx in range(1, nx):
        start(functools.partial(x_copy, dx, 2))
    recvx[2, x] = sendx[2]
    for dx in range(1, nx):
        x_wait(dx, 2)
    sums = recvx[2, 0]
    for xx in range(1, nx):
        sums += recvx[2, xx]
    sums = jnp.broadcast_to(jnp.sum(sums, axis=1, keepdims=True), (8, LANES))
    norm2 = [sums[q : q + 1] for q in range(POLS)]
    inverse = spread([1.0 / jnp.sqrt(t) for t in norm2])
    for g in range(8):
        value = last[g] * inverse
        for q in range(POLS):
            for t in range(QUARTERS):
                at = (t * 8 + g) * LANES
                last_ref[q : q + 1, at : at + LANES] = value[4 * q + t : 4 * q + t + 1, :]
    for q in range(POLS):
        alpha_ref[q : q + 1, 0:1] = alpha0[q][:, :1]
        alpha_ref[q : q + 1, 1:2] = alpha1[q][:, :1]
        beta_ref[q : q + 1, 0:1] = jnp.sqrt(ratio[q])[:, :1]
        beta_ref[q : q + 1, 1:2] = jnp.sqrt(norm2[q] / norm1[q])[:, :1]

    finish()


def lanczos(sizes, kernel_half, dipole, band_energy, core_energy, core_index):
    nx, nz, _ = sizes
    rows, cols = kernel_half.shape
    dma = pltpu.SemaphoreType.DMA
    chunk = (ROWS, LANES)
    return pl.pallas_call(
        functools.partial(kernel, sizes),
        out_shape=(
            jax.ShapeDtypeStruct((POLS, 2), F32),
            jax.ShapeDtypeStruct((POLS, 2), F32),
            jax.ShapeDtypeStruct(dipole.shape, F32),
        ),
        in_specs=[pl.BlockSpec(memory_space=pl.ANY)] * 5,
        out_specs=[pl.BlockSpec(memory_space=pltpu.VMEM)] * 3,
        scratch_shapes=[
            pltpu.VMEM((rows, cols), BF),
            pltpu.VMEM(dipole.shape, F32),
            pltpu.VMEM(band_energy.shape, F32),
            pltpu.SMEM(core_energy.shape, F32),
            pltpu.SMEM(core_index.shape, jnp.int32),
            pltpu.VMEM((POLS, cols), F32),
            pltpu.VMEM((2, 8, *chunk), F32),
            pltpu.VMEM((8, *chunk), F32),
            pltpu.VMEM((2 * ROWS, 8 * LANES), BF),
            pltpu.VMEM((2, 4, 2, *chunk), F32),
            pltpu.VMEM((2, 8, *chunk), F32),
            pltpu.VMEM((2, 2, *chunk), F32),
            pltpu.VMEM((2, nx, *chunk), F32),
            pltpu.VMEM((2, *chunk), F32),
            pltpu.VMEM((2, nz, *chunk), F32),
            pltpu.VMEM((2, *chunk), F32),
            pltpu.VMEM((2, 8, *chunk), F32),
            pltpu.VMEM((2, *chunk), F32),
            pltpu.VMEM((3, 8, LANES), F32),
            pltpu.VMEM((3, nx, 8, LANES), F32),
            dma((6,)), dma((2,)),
            dma((nx - 1,)), dma((1,)),
            dma((2, 4, 2)), dma((2, 8)),
            dma((2, 2)), dma((2, nx)),
            dma((2, nz - 1)), dma((2, nz)),
            dma((2, 7)), dma((2, 8)),
            dma((nx - 1,)), dma((2,)),
            dma((3, nx - 1)), dma((3, nx)),
        ],
        compiler_params=pltpu.CompilerParams(collective_id=0, has_side_effects=True),
    )(kernel_half, dipole, band_energy, core_energy, core_index)


def solution(mesh):
    nx, np_, nz = mesh.shape["row"], mesh.shape["pol"], mesh.shape["col"] // 4
    sizes = (nx, nz, nz * np_ // nx)
    in_specs = (P("row", ("pol", "col")), P(None, "row"), P("row", None), P(), P("row"))
    out_specs = (P(), P(), P(None, "row"))
    return jax.shard_map(
        functools.partial(lanczos, sizes), mesh=mesh, in_specs=in_specs, out_specs=out_specs, check_vma=False
    )
```

time: 173 us -> 48.7 us (0.28)
  waiting for transfers between devices: 76.1 us -> 0 us
  starting transfers between devices: 52.3 us -> 0 us
  Pallas kernels: 0 us -> 43.7 us
  blocking collectives: 28.9 us -> 0 us
  other arithmetic: 4.85 us -> 0 us
  local copies, waits for them, and re-layouts: 6.83 us -> 4.11 us
  matrix products: 2.03 us -> 0 us
    all_to_all x9 -> x0, waiting for transfers between devices: 76.1 us -> none  [the longest x7 57.5 us: copy_for_each(): lax.all_to_all(jnp.broadcast_to(x[None], (count, *x.shape)), axis, 0, 0,...]
    all_to_all x9 -> x0, starting transfers between devices: 52.3 us -> none  [the longest x7 29.9 us: copy_for_each(): lax.all_to_all(jnp.broadcast_to(x[None], (count, *x.shape)), axis, 0, 0,...]
    pallas_call x0 -> x1, Pallas kernels: none -> 43.7 us  [lanczos(): pl.pallas_call(functools.partial(kernel, sizes), out_shape=(jax.ShapeDtyp...]
    all_to_all x4 -> x0, blocking collectives: 28.9 us -> none  [copy_for_each(): lax.all_to_all(jnp.broadcast_to(x[None], (count, *x.shape)), axis, 0, 0,...]
    broadcast_in_dim x11 -> x0, local copies, waits for them, and re-layouts: 4.73 us -> none  [copy_for_each(): jnp.broadcast_to(x[None], (count, *x.shape))]
    pallas_call x0 -> x2, local copies, waits for them, and re-layouts: none -> 2.63 us  [lanczos(): pl.pallas_call(functools.partial(kernel, sizes), out_shape=(jax.ShapeDtyp...]
    dot_general x4 -> x0, matrix products: 2.03 us -> none  [the longest x2 1.27 us: local(): lax.dot_general(picked, kernel_half, (((1,), (1,)), ((), ())), preferred_...]
    reduce_sum x11 -> x0, other arithmetic: 1.96 us -> none  [the longest x1 1.14 us: local(): start_sq = over_copies(jnp.sum(dipole * dipole, axis=1), 'row')]
  transfers between devices with their start and end apart: 9 -> 0, of which waited for: 9 -> 0; matrix products, arithmetic and copies ran while one was open for 1% -> 0% of each run, Pallas kernels for 0% -> 0%
where the time goes in v1:
time: 48.7 us; the launch traced here: 48.5 us
  Pallas kernels  43.7 us (90%)
  local copies, waits for them, and re-layouts  4.11 us (8%)
  between operations  0.64 us (1%)
    pallas_call x1, Pallas kernels, lanczos(): pl.pallas_call(functools.partial(kernel, sizes), out_shape=(jax.ShapeDtyp...  43.7 us
    pallas_call x2, local copies, waits for them, and re-layouts, lanczos(): pl.pallas_call(functools.partial(kernel, sizes), out_shape=(jax.ShapeDtyp...  2.63 us
    unnamed x1, local copies, waits for them, and re-layouts  1.48 us

profile of v1, /device:TPU:1, one launch (start us, length us, event | category | flops | bytes accessed | tf_op | source)
XLA Modules:
  0.0 48.5 jit_solution(15429070496062456311)
XLA Ops:
  0.6 43.7 %shard_map.76 = (f32[3,2]{1,0:T(4,128)}, f32[3,2]{1,0:T(4,128)}, f32[3,4096]{1,0:T(4,128)}) custom-call(bf16[4096,256]{1,0:T(8,128)(2,1)} %w_hbm.1, f32[3,4096]{1,0:T(4,128)} %dip_hbm.1, f32[2,512]{1,0:T(2,128)} %band_hbm.1, f32[4]{0:T(128)} %core_hbm.1, s32[8]{0:T(128)} %index_hbm.1), custom_call_target="tpu_custom_call" | custom-call | tf_op jit(solution)/shard_map/pallas_call | solution.py:430
  44.4 1.3 %copy.8 = f32[3,2]{0,1:T(2,128)} copy(f32[3,2]{1,0:T(4,128)} %get-tuple-element.3) | data formatting | bytes 48 | tf_op jit(solution)/shard_map/pallas_call | solution.py:430
  45.7 1.3 %copy.9 = f32[3,2]{0,1:T(2,128)} copy(f32[3,2]{1,0:T(4,128)} %get-tuple-element.4) | data formatting | bytes 48 | tf_op jit(solution)/shard_map/pallas_call | solution.py:430
  47.0 1.5 %copy.11 = f32[3,4096]{1,0:T(4,128)} copy(f32[3,4096]{1,0:T(4,128)} %get-tuple-element.11) | data formatting | bytes 98304

commit v2 on v0

v2 whole, which is shorter than its diff:
```python
import functools

import jax
import jax.numpy as jnp
from jax import lax
from jax.experimental import pallas as pl
from jax.experimental.pallas import tpu as pltpu
from jax.sharding import PartitionSpec as P

F32 = jnp.float32
BF = jnp.bfloat16
MESH = pl.DeviceIdType.MESH
CORES = 4
LANES = 128
POLS = 3
LINES = 8
ROWS = POLS * LINES


def spread(parts):
    return jnp.concatenate([jnp.broadcast_to(t, (LINES, t.shape[1])) for t in parts], axis=0)


def over_lines(x):
    return [jnp.sum(x[LINES * q : LINES * (q + 1)], axis=0, keepdims=True) for q in range(POLS)]


def placed(parts, first=0):
    row = lax.broadcasted_iota(jnp.int32, (8, LANES), 0)
    out = jnp.zeros((8, LANES), F32)
    for q, part in enumerate(parts):
        out = jnp.where(row == first + q, jnp.broadcast_to(part, (8, LANES)), out)
    return out


def two_terms(x):
    high = x.astype(BF).astype(F32)
    return jnp.concatenate([high, x - high], axis=0).astype(BF)


def joined(x):
    return x[:ROWS] + x[ROWS:]


def kernel(
    sizes,
    w_hbm, dip_hbm, band_hbm, core_hbm, index_hbm,
    alpha_ref, beta_ref, last_ref,
    w, dip, band, core, index,
    uc0, u, en,
    send1, recv1, sendc, recvc, send2, recv2, send3, recv3, sendt, recvt, sendx, recvx, sendn, recvn,
    load_sem, core_sem, s0, r0, s1, r1, sc, rc, s2, r2, s3, r3, st, rt, sx, rx, sn, rn,
):
    nx, nz, zl_count = sizes
    zh_count = nz // zl_count
    p = lax.axis_index("pol")
    x = lax.axis_index("row")
    col = lax.axis_index("col")
    z = col // 4
    h = (col // 2) % 2
    k = col % 2
    y = h * 2 + p
    zl = z % zl_count
    home = p * zh_count + z // zl_count
    is_home = x == home
    away = jnp.logical_not(is_home)
    owner = k == 1
    keeper = (z // zl_count) == (x % zh_count)
    p_keep = x // zh_count

    def dev(pp, xx, zz, hh, kk):
        return (pp, xx, zz * 4 + hh * 2 + kk)

    barrier = pltpu.get_barrier_semaphore()

    def greet(d):
        pl.semaphore_signal(barrier, inc=1, device_id=d, device_id_type=MESH)

    beside = [(dx, j) for dx in (2, 1, 3, 0) for j in range(4)]
    for dx, j in beside:
        hh, pp = (h + j // 2) % 2, (p + j % 2) % 2
        if (dx, j) == (0, 0):
            greet(dev(p, x, z, h, 1 - k))
        else:
            greet(dev(pp, (x + dx) % nx, z, hh, 1))

    @pl.when(owner)
    def _():
        for d in sorted(range(1, nz), key=lambda d: -min(d, nz - d)):
            greet(dev(p, x, (z + d) % nz, h, 1))
        for dx, j in beside:
            if (dx, j) != (0, 0):
                greet(dev((p + j % 2) % 2, (x + dx) % nx, z, (h + j // 2) % 2, 0))

    loads = [
        pltpu.make_async_copy(dip_hbm, dip, load_sem.at[0]),
        pltpu.make_async_copy(band_hbm, band, load_sem.at[1]),
        pltpu.make_async_copy(core_hbm, core, core_sem.at[0]),
        pltpu.make_async_copy(index_hbm, index, core_sem.at[1]),
    ]
    for c in loads:
        c.start()
    big = w.shape[0] // 4
    w_loads = [
        pltpu.make_async_copy(
            w_hbm.at[pl.ds(i * big, big)], w.at[pl.ds(i * big, big)], load_sem.at[2 + i]
        )
        for i in range(4)
    ]
    for c in w_loads:
        c.start()

    ends = []

    def start(make, condition=None, within=None):
        if condition is None:
            make().start()
        else:
            pl.when(condition)(lambda: make().start())
        ends.append((make, condition, within))

    def finish():
        for make, condition, within in ends:
            if condition is None and within is None:
                make().wait_send()
            elif condition is None or within is None:
                pl.when(within if condition is None else condition)(lambda make=make: make().wait_send())
            else:
                pl.when(jnp.logical_and(condition, within))(lambda make=make: make().wait_send())

    def send(src, dst, send_sem, recv_sem, device):
        return pltpu.make_async_remote_copy(
            src_ref=src, dst_ref=dst, send_sem=send_sem, recv_sem=recv_sem, device_id=device,
            device_id_type=MESH,
        )

    me = dev(p, x, z, h, k)

    def arrived(dst, recv_sem, spare_sem):
        send(dst, dst, spare_sem, recv_sem, me).wait_recv()

    for c in loads:
        c.wait()
    for c in range(4):
        for q in range(POLS):
            for t in range(LINES):
                at = ((t // 2) * 8 + (c // 2) * 4 + (t % 2) * 2 + c % 2) * LANES
                u[0, c, LINES * q + t : LINES * q + t + 1, :] = dip[q : q + 1, at : at + LANES]
    offsets = []
    for i in range(2 * CORES):
        level = index[i]
        off = jnp.float32(0.0)
        for j in range(CORES):
            off = jnp.where(level == j, core[j], off)
        offsets.append(off)
    row8 = lax.broadcasted_iota(jnp.int32, (8, LANES), 0)
    for c in range(4):
        value = jnp.zeros((8, LANES), F32)
        for t in range(LINES):
            line = (t // 2) * 8 + (c // 2) * 4 + (t % 2) * 2 + c % 2
            at = (line % 4) * LANES
            level = band[line // 16 : line // 16 + 1, at : at + LANES] - offsets[line // 4]
            value = jnp.where(row8 == t, jnp.broadcast_to(level, (8, LANES)), value)
        en[c] = value

    pl.semaphore_wait(barrier, jnp.where(owner, 2 * len(beside) - 1 + nz - 1, len(beside)))

    def own_lines(kk):
        return pl.ds(pl.multiple_of((zl * 4 + h * 2 + kk) * 2 * LANES, 2 * LANES), 2 * LANES)

    def first_copy(dx, kk):
        return send(
            dip.at[:, own_lines(kk)], uc0, s0.at[dx - 1, kk], r0.at[0], dev(p, (x + dx) % nx, z, h, kk)
        )

    for dx in (2, 1, 3):
        for kk in range(2):
            start(functools.partial(first_copy, dx, kk), jnp.logical_and(is_home, owner))

    @pl.when(is_home)
    def _():
        uc0[...] = dip[:, own_lines(k)]

    for c in w_loads:
        c.wait()

    row_mod = lax.broadcasted_iota(jnp.int32, (ROWS, 2 * LANES), 0) % LINES

    def line_rows(hh, pp, t):
        line = (t // 2) * 8 + hh * 4 + (t % 2) * 2 + pp
        return pl.ds(pl.multiple_of(line * LANES, LANES), LANES)

    def columns_of(value, hh, pp):
        left = two_terms(value)
        out = jnp.zeros((ROWS, 2 * LANES), F32)
        for t in range(LINES):
            part = joined(jnp.dot(left, w[line_rows(hh, pp, t), :], preferred_element_type=F32))
            out = jnp.where(row_mod == t, part, out)
        return out

    near = [(0, 0), (0, 1), (1, 1), (1, 0)]

    alpha = ratio = column = col_first = norms = None
    for step in range(2):
        rows = ROWS + 8 if step == 0 else ROWS
        sums = jnp.zeros((ROWS, 2 * LANES), F32)
        if step == 0:
            for c in range(4):
                sums += columns_of(u[0, c], c // 2, c % 2)
            col_part = over_lines(sums)
            col_first = col_part
        else:
            for jh, jp in near:
                hh, pp = (h + jh) % 2, (p + jp) % 2
                c = hh * 2 + pp
                hear = functools.partial(arrived, recv3.at[0, c], r3.at[0, c], s3.at[0, 0])
                if (jh, jp) == (0, 0):
                    pl.when(jnp.logical_not(owner))(hear)
                else:
                    hear()
                sums += columns_of(recv3[0, c], hh, pp)
            for xx in range(nx):
                pl.when(jnp.logical_not(jnp.logical_and(owner, x == xx)))(
                    functools.partial(arrived, recvx.at[0, xx], rx.at[0, xx], sx.at[0, 0])
                )
            whole = recvx[0, 0]
            for xx in range(1, nx):
                whole += recvx[0, xx]
            whole = jnp.broadcast_to(jnp.sum(whole, axis=1, keepdims=True), (8, LANES))
            norms = [whole[q : q + 1] for q in range(POLS)]
            alpha = [whole[4 + q : 5 + q] / norms[q] for q in range(POLS)]
            col_part = over_lines(sums)
            col_part = [col_part[q] - alpha[q][:, :1] * col_first[q] for q in range(POLS)]
        for half in range(2):
            sendc[step, half] = placed([t[:, half * LANES : (half + 1) * LANES] for t in col_part])

        def col_copy(half, step=step):
            return send(
                sendc.at[step, half], recvc.at[step, x, k], sc.at[step, half], rc.at[step, x, k],
                dev(half, home, z, h, 1),
            )

        for half in range(2):
            mine = jnp.logical_and(owner, jnp.logical_and(is_home, p == half))

            @pl.when(mine)
            def _(half=half, step=step):
                recvc[step, x, k] = sendc[step, half]

            start(functools.partial(col_copy, half), jnp.logical_not(mine))

        if step == 0:
            pl.when(away)(functools.partial(arrived, uc0, r0.at[0], s0.at[0, 0]))
            column = [uc0[q : q + 1, :] for q in range(POLS)]
        else:

            @pl.when(is_home)
            def _():
                for half in range(2):
                    value = recv3[0, h * 2 + half]
                    mask = lax.broadcasted_iota(jnp.int32, (ROWS, LANES), 0) % LINES == zl * 2 + k
                    recvt[half] = placed(over_lines(jnp.where(mask, value, 0.0)))

            for half in range(2):
                pl.when(away)(functools.partial(arrived, recvt.at[half], rt.at[half], st.at[0, 0]))
            got = jnp.concatenate([recvt[0], recvt[1]], axis=1)
            got = jnp.where(away, jnp.where(k == 1, pltpu.roll(got, 4, 0), got), got)
            column = [got[q : q + 1] - alpha[q][:, :1] * column[q] for q in range(POLS)]
        if step == 0:
            twice = []
            for q in range(POLS):
                line = 2.0 * col_part[q] * column[q]
                twice.append(line[:, :LANES] + line[:, LANES:])
            sum_rows = placed(twice)
        left = two_terms(spread(column))

        def row_copy(j, step=step, rows=rows):
            jh, jp = near[j]
            return send(
                send1.at[step, j, pl.ds(0, rows)], recv1.at[step, y * 2 + k, pl.ds(0, rows)],
                s1.at[step, j], r1.at[step, y * 2 + k], dev((p + jp) % 2, x, z, (h + jh) % 2, 1),
            )

        for j in (3, 2, 1, 0):
            jh, jp = near[j]
            hh, pp = (h + jh) % 2, (p + jp) % 2
            lines = jnp.zeros((ROWS, LANES), F32)
            for t in range(LINES):
                part = joined(
                    lax.dot_general(
                        left, w[line_rows(hh, pp, t), :], (((1,), (1,)), ((), ())),
                        preferred_element_type=F32,
                    )
                )
                lines = jnp.where(row_mod[:, :LANES] == t, part, lines)
            send1[step, j, :ROWS] = lines
            if step == 0:
                send1[step, j, ROWS:] = sum_rows
            start(functools.partial(row_copy, j), None if j else jnp.logical_not(owner))

        if step == 1:
            factor = spread(alpha)
            for c in range(4):
                u[1, c] = recv3[0, c] - factor * u[0, c]
        squares = jnp.zeros((ROWS, LANES), F32)
        weighted = jnp.zeros((ROWS, LANES), F32)
        for c in range(4):
            sq = u[step, c] * u[step, c]
            squares += sq
            weighted += jnp.concatenate([en[c]] * POLS, axis=0) * sq
        own_sums = placed(over_lines(squares))

        def x_copy(dx, kk, at):
            return send(
                sendx.at[at], recvx.at[at, x], sx.at[at, (dx - 1) * 2 + kk if dx else 6], rx.at[at, x],
                dev(p, (x + dx) % nx, z, h, kk),
            )

        def share(at):
            for dx in (2, 1, 3):
                for kk in range(2):
                    start(functools.partial(x_copy, dx, kk, at), None, owner)
            start(functools.partial(x_copy, 0, 0, at), None, owner)
            recvx[at, x] = sendx[at]

        if step == 0:
            own_sums += placed(over_lines(weighted), 4)

        @pl.when(owner)
        def _(step=step, rows=rows, own_sums=own_sums):
            if step == 1:
                sendx[1] = own_sums
                share(1)
            recv1[step, y * 2 + k, pl.ds(0, rows)] = send1[step, 0, pl.ds(0, rows)]
            for jh, jp in near:
                hh, pp = (h + jh) % 2, (p + jp) % 2
                for kk in range(2):
                    if (jh, jp, kk) != (0, 0, 1):
                        g = (hh * 2 + pp) * 2 + kk
                        arrived(recv1.at[step, g, pl.ds(0, rows)], r1.at[step, g], s1.at[step, 0])
            total = recv1[step, 0, pl.ds(0, rows)]
            for g in range(1, 8):
                total += recv1[step, g, pl.ds(0, rows)]
            send2[step, pl.ds(0, rows)] = total

            @pl.when(keeper)
            def _():
                for kk in range(2):
                    for xx in range(nx):
                        hear = functools.partial(
                            arrived, recvc.at[step, xx, kk], rc.at[step, xx, kk], sc.at[step, 0]
                        )
                        if kk == 0:
                            hear()
                        else:
                            pl.when(jnp.logical_not(jnp.logical_and(x == xx, p == p_keep)))(hear)
                    cols = recvc[step, 0, kk]
                    for xx in range(1, nx):
                        cols += recvc[step, xx, kk]
                    for q in range(POLS):
                        at = pl.ds(LINES * q, LINES)
                        line = jnp.broadcast_to(cols[q : q + 1], (8, LANES))
                        send2[step, at] = send2[step, at] + jnp.where(row8 == zl * 2 + kk, line, 0.0)

            def z_copy(d):
                return send(
                    send2.at[step, pl.ds(0, rows)], recv2.at[step, z, pl.ds(0, rows)], s2.at[step, d - 1],
                    r2.at[step, z], dev(p, x, (z + d) % nz, h, 1),
                )

            for d in sorted(range(1, nz), key=lambda d: -min(d, nz - d)):
                start(functools.partial(z_copy, d), None, owner)
            recv2[step, z, pl.ds(0, rows)] = send2[step, pl.ds(0, rows)]
            if step == 1:
                for dx in range(1, nx):
                    xx = (x + dx) % nx
                    arrived(recvx.at[1, xx], rx.at[1, xx], sx.at[1, 0])
            for d in range(1, nz):
                zz = (z + d) % nz
                arrived(recv2.at[step, zz, pl.ds(0, rows)], r2.at[step, zz], s2.at[step, 0])
            total = recv2[step, 0, pl.ds(0, rows)]
            for zz in range(1, nz):
                total += recv2[step, zz, pl.ds(0, rows)]
            value = total[:ROWS] + jnp.concatenate([en[y]] * POLS, axis=0) * u[step, y]

            if step == 0:
                sendx[0] = jnp.concatenate([total[ROWS + 4 :], total[ROWS : ROWS + 4]], axis=0) + own_sums
                share(0)
                send3[0] = value
                mod = lax.broadcasted_iota(jnp.int32, (ROWS, LANES), 0) % LINES
                tile = jnp.zeros((8, LANES), F32)
                for kk in range(2):
                    tile += placed(over_lines(jnp.where(mod == zl * 2 + kk, value, 0.0)), 4 * kk)
                sendt[...] = tile

                def tile_copy(dx, kk):
                    return send(
                        sendt, recvt.at[p], st.at[dx - 1, kk], rt.at[p],
                        dev(p_keep, (x + dx) % nx, z, h, kk),
                    )

                for dx in (2, 1, 3):
                    for kk in range(2):
                        start(functools.partial(tile_copy, dx, kk), keeper, owner)
            else:
                w1 = value - spread(alpha) * u[1, y] - spread(ratio_of(1)) * u[0, y]
                sendn[...] = placed(over_lines(w1 * w1)) + placed(over_lines(w1 * u[1, y]), 4)

                def sums_copy(dx, j, kk):
                    jh, jp = near[j]
                    return send(
                        sendn, recvn.at[x, y], sn.at[dx, j, kk], rn.at[x, y],
                        dev((p + jp) % 2, (x + dx) % nx, z, (h + jh) % 2, kk),
                    )

                for dx in (2, 1, 3, 0):
                    for j in (3, 2, 1, 0):
                        for kk in range(2):
                            if (dx, j, kk) != (0, 0, 1):
                                start(functools.partial(sums_copy, dx, j, kk), None, owner)
                recvn[x, y] = sendn[...]
                send3[1] = w1

            def chunk_copy(j, kk):
                jh, jp = near[j]
                return send(
                    send3.at[step], recv3.at[step, y], s3.at[step, j * 2 + kk], r3.at[step, y],
                    dev((p + jp) % 2, x, z, (h + jh) % 2, kk),
                )

            for j in (3, 2, 1, 0):
                for kk in range(2):
                    if (j, kk) != (0, 1):
                        start(functools.partial(chunk_copy, j, kk), None, owner)
            recv3[step, y] = send3[step]

        def ratio_of(at):
            whole = recvx[at, 0]
            for xx in range(1, nx):
                whole += recvx[at, xx]
            whole = jnp.broadcast_to(jnp.sum(whole, axis=1, keepdims=True), (8, LANES))
            return [whole[q : q + 1] / norms[q] for q in range(POLS)]

    @pl.when(jnp.logical_not(owner))
    def _():
        for xx in range(nx):
            arrived(recvx.at[1, xx], rx.at[1, xx], sx.at[1, 0])

    ratio = ratio_of(1)
    norm1 = [ratio[q] * norms[q] for q in range(POLS)]
    for xx in range(nx):
        for c in range(4):
            pl.when(jnp.logical_not(jnp.logical_and(owner, jnp.logical_and(x == xx, y == c))))(
                functools.partial(arrived, recvn.at[xx, c], rn.at[xx, c], sn.at[0, 0, 0])
            )
    whole = jnp.zeros((8, LANES), F32)
    for xx in range(nx):
        for c in range(4):
            whole += recvn[xx, c]
    whole = jnp.broadcast_to(jnp.sum(whole, axis=1, keepdims=True), (8, LANES))
    shift = [whole[4 + q : 5 + q] / norm1[q] for q in range(POLS)]
    norm2 = [whole[q : q + 1] - shift[q] * whole[4 + q : 5 + q] for q in range(POLS)]
    inverse = spread([1.0 / jnp.sqrt(t) for t in norm2])
    back = spread(shift)
    for jh, jp in near:
        c = (h + jh) % 2 * 2 + (p + jp) % 2
        hear = functools.partial(arrived, recv3.at[1, c], r3.at[1, c], s3.at[1, 0])
        if (jh, jp) == (0, 0):
            pl.when(jnp.logical_not(owner))(hear)
        else:
            hear()
    for c in range(4):
        value = (recv3[1, c] - back * u[1, c]) * inverse
        for q in range(POLS):
            for t in range(LINES):
                at = ((t // 2) * 8 + (c // 2) * 4 + (t % 2) * 2 + c % 2) * LANES
                last_ref[q : q + 1, at : at + LANES] = value[LINES * q + t : LINES * q + t + 1, :]
    for q in range(POLS):
        alpha_ref[q : q + 1, 0:1] = alpha[q][:, :1]
        alpha_ref[q : q + 1, 1:2] = (alpha[q] + shift[q])[:, :1]
        beta_ref[q : q + 1, 0:1] = jnp.sqrt(ratio[q])[:, :1]
        beta_ref[q : q + 1, 1:2] = jnp.sqrt(norm2[q] / norm1[q])[:, :1]
    finish()


def lanczos(sizes, kernel_half, dipole, band_energy, core_energy, core_index):
    nx, nz, _ = sizes
    rows, cols = kernel_half.shape
    dma = pltpu.SemaphoreType.DMA
    chunk = (ROWS, LANES)
    longer = (ROWS + 8, LANES)
    tile = (8, LANES)
    return pl.pallas_call(
        functools.partial(kernel, sizes),
        out_shape=(
            jax.ShapeDtypeStruct((POLS, 2), F32),
            jax.ShapeDtypeStruct((POLS, 2), F32),
            jax.ShapeDtypeStruct(dipole.shape, F32),
        ),
        in_specs=[pl.BlockSpec(memory_space=pl.ANY)] * 5,
        out_specs=[pl.BlockSpec(memory_space=pltpu.VMEM)] * 3,
        scratch_shapes=[
            pltpu.VMEM((rows, cols), BF),
            pltpu.VMEM(dipole.shape, F32),
            pltpu.VMEM(band_energy.shape, F32),
            pltpu.SMEM(core_energy.shape, F32),
            pltpu.SMEM(core_index.shape, jnp.int32),
            pltpu.VMEM((POLS, cols), F32),
            pltpu.VMEM((2, 4, *chunk), F32),
            pltpu.VMEM((4, *tile), F32),
            pltpu.VMEM((2, 4, *longer), F32),
            pltpu.VMEM((2, 8, *longer), F32),
            pltpu.VMEM((2, 2, *tile), F32),
            pltpu.VMEM((2, nx, 2, *tile), F32),
            pltpu.VMEM((2, *longer), F32),
            pltpu.VMEM((2, nz, *longer), F32),
            pltpu.VMEM((2, *chunk), F32),
            pltpu.VMEM((2, 4, *chunk), F32),
            pltpu.VMEM(tile, F32),
            pltpu.VMEM((2, *tile), F32),
            pltpu.VMEM((2, *tile), F32),
            pltpu.VMEM((2, nx, *tile), F32),
            pltpu.VMEM(tile, F32),
            pltpu.VMEM((nx, 4, *tile), F32),
            dma((6,)), dma((2,)),
            dma((nx - 1, 2)), dma((1,)),
            dma((2, 4)), dma((2, 8)),
            dma((2, 2)), dma((2, nx, 2)),
            dma((2, nz - 1)), dma((2, nz)),
            dma((2, 8)), dma((2, 4)),
            dma((nx - 1, 2)), dma((2,)),
            dma((2, 7)), dma((2, nx)),
            dma((nx, 4, 2)), dma((nx, 4)),
        ],
        compiler_params=pltpu.CompilerParams(collective_id=0, has_side_effects=True),
    )(kernel_half, dipole, band_energy, core_energy, core_index)


def solution(mesh):
    nx, np_, nz = mesh.shape["row"], mesh.shape["pol"], mesh.shape["col"] // 4
    sizes = (nx, nz, nz * np_ // nx)
    in_specs = (P("row", ("pol", "col")), P(None, "row"), P("row", None), P(), P("row"))
    out_specs = (P(), P(), P(None, "row"))
    return jax.shard_map(
        functools.partial(lanczos, sizes), mesh=mesh, in_specs=in_specs, out_specs=out_specs, check_vma=False
    )
```

time: 173 us -> 43.7 us (0.25)
  waiting for transfers between devices: 76.1 us -> 0 us
  starting transfers between devices: 52.3 us -> 0 us
  Pallas kernels: 0 us -> 38.8 us
  blocking collectives: 28.9 us -> 0 us
  other arithmetic: 4.85 us -> 0 us
  local copies, waits for them, and re-layouts: 6.83 us -> 4.11 us
  matrix products: 2.03 us -> 0 us
    all_to_all x9 -> x0, waiting for transfers between devices: 76.1 us -> none  [the longest x7 57.5 us: copy_for_each(): lax.all_to_all(jnp.broadcast_to(x[None], (count, *x.shape)), axis, 0, 0,...]
    all_to_all x9 -> x0, starting transfers between devices: 52.3 us -> none  [the longest x7 29.9 us: copy_for_each(): lax.all_to_all(jnp.broadcast_to(x[None], (count, *x.shape)), axis, 0, 0,...]
    pallas_call x0 -> x1, Pallas kernels: none -> 38.8 us  [lanczos(): pl.pallas_call(functools.partial(kernel, sizes), out_shape=(jax.ShapeDtyp...]
    all_to_all x4 -> x0, blocking collectives: 28.9 us -> none  [copy_for_each(): lax.all_to_all(jnp.broadcast_to(x[None], (count, *x.shape)), axis, 0, 0,...]
    broadcast_in_dim x11 -> x0, local copies, waits for them, and re-layouts: 4.73 us -> none  [copy_for_each(): jnp.broadcast_to(x[None], (count, *x.shape))]
    pallas_call x0 -> x2, local copies, waits for them, and re-layouts: none -> 2.63 us  [lanczos(): pl.pallas_call(functools.partial(kernel, sizes), out_shape=(jax.ShapeDtyp...]
    dot_general x4 -> x0, matrix products: 2.03 us -> none  [the longest x2 1.27 us: local(): lax.dot_general(picked, kernel_half, (((1,), (1,)), ((), ())), preferred_...]
    reduce_sum x11 -> x0, other arithmetic: 1.96 us -> none  [the longest x1 1.14 us: local(): start_sq = over_copies(jnp.sum(dipole * dipole, axis=1), 'row')]
  transfers between devices with their start and end apart: 9 -> 0, of which waited for: 9 -> 0; matrix products, arithmetic and copies ran while one was open for 1% -> 0% of each run, Pallas kernels for 0% -> 0%
where the time goes in v2:
time: 43.7 us; the launch traced here: 43.5 us
  Pallas kernels  38.8 us (89%)
  local copies, waits for them, and re-layouts  4.11 us (9%)
  between operations  0.64 us (1%)
    pallas_call x1, Pallas kernels, lanczos(): pl.pallas_call(functools.partial(kernel, sizes), out_shape=(jax.ShapeDtyp...  38.8 us
    pallas_call x2, local copies, waits for them, and re-layouts, lanczos(): pl.pallas_call(functools.partial(kernel, sizes), out_shape=(jax.ShapeDtyp...  2.63 us
    unnamed x1, local copies, waits for them, and re-layouts  1.48 us

profile of v2, /device:TPU:1, one launch (start us, length us, event | category | flops | bytes accessed | tf_op | source)
XLA Modules:
  0.0 43.5 jit_solution(5538541538662773763)
XLA Ops:
  0.6 38.8 %shard_map.76 = (f32[3,2]{1,0:T(4,128)}, f32[3,2]{1,0:T(4,128)}, f32[3,4096]{1,0:T(4,128)}) custom-call(bf16[4096,256]{1,0:T(8,128)(2,1)} %w_hbm.1, f32[3,4096]{1,0:T(4,128)} %dip_hbm.1, f32[2,512]{1,0:T(2,128)} %band_hbm.1, f32[4]{0:T(128)} %core_hbm.1, s32[8]{0:T(128)} %index_hbm.1), custom_call_target="tpu_custom_call" | custom-call | tf_op jit(solution)/shard_map/pallas_call | solution.py:493
  39.4 1.3 %copy.8 = f32[3,2]{0,1:T(2,128)} copy(f32[3,2]{1,0:T(4,128)} %get-tuple-element.3) | data formatting | bytes 48 | tf_op jit(solution)/shard_map/pallas_call | solution.py:493
  40.7 1.3 %copy.9 = f32[3,2]{0,1:T(2,128)} copy(f32[3,2]{1,0:T(4,128)} %get-tuple-element.4) | data formatting | bytes 48 | tf_op jit(solution)/shard_map/pallas_call | solution.py:493
  42.0 1.5 %copy.11 = f32[3,4096]{1,0:T(4,128)} copy(f32[3,4096]{1,0:T(4,128)} %get-tuple-element.11) | data formatting | bytes 98304

commit v3 on v2

--- a/solution.py
+++ b/solution.py
@@ -476,11 +476,20 @@
                 at = ((t // 2) * 8 + (c // 2) * 4 + (t % 2) * 2 + c % 2) * LANES
                 last_ref[q : q + 1, at : at + LANES] = value[LINES * q + t : LINES * q + t + 1, :]
     for q in range(POLS):
-        alpha_ref[q : q + 1, 0:1] = alpha[q][:, :1]
-        alpha_ref[q : q + 1, 1:2] = (alpha[q] + shift[q])[:, :1]
-        beta_ref[q : q + 1, 0:1] = jnp.sqrt(ratio[q])[:, :1]
-        beta_ref[q : q + 1, 1:2] = jnp.sqrt(norm2[q] / norm1[q])[:, :1]
+        alpha_ref[0:1, q : q + 1] = alpha[q][:, :1]
+        alpha_ref[1:2, q : q + 1] = (alpha[q] + shift[q])[:, :1]
+        beta_ref[0:1, q : q + 1] = jnp.sqrt(ratio[q])[:, :1]
+        beta_ref[1:2, q : q + 1] = jnp.sqrt(norm2[q] / norm1[q])[:, :1]
     finish()
+
+
+def write_out(*refs):
+    sources, targets, sems = refs[:3], refs[3:6], refs[6]
+    copies = [pltpu.make_async_copy(a, b, sems.at[i]) for i, (a, b) in enumerate(zip(sources, targets, strict=True))]
+    for c in copies:
+        c.start()
+    for c in copies:
+        c.wait()
 
 
 def lanczos(sizes, kernel_half, dipole, band_energy, core_energy, core_index):
@@ -490,13 +499,9 @@
     chunk = (ROWS, LANES)
     longer = (ROWS + 8, LANES)
     tile = (8, LANES)
-    return pl.pallas_call(
+    results = pl.pallas_call(
         functools.partial(kernel, sizes),
-        out_shape=(
-            jax.ShapeDtypeStruct((POLS, 2), F32),
-            jax.ShapeDtypeStruct((POLS, 2), F32),
-            jax.ShapeDtypeStruct(dipole.shape, F32),
-        ),
+        out_shape=(pltpu.VMEM((2, POLS), F32), pltpu.VMEM((2, POLS), F32), pltpu.VMEM(dipole.shape, F32)),
         in_specs=[pl.BlockSpec(memory_space=pl.ANY)] * 5,
         out_specs=[pl.BlockSpec(memory_space=pltpu.VMEM)] * 3,
         scratch_shapes=[
@@ -534,6 +539,18 @@
         ],
         compiler_params=pltpu.CompilerParams(collective_id=0, has_side_effects=True),
     )(kernel_half, dipole, band_energy, core_energy, core_index)
+    alphas, betas, last = pl.pallas_call(
+        write_out,
+        out_shape=(
+            jax.ShapeDtypeStruct((2, POLS), F32),
+            jax.ShapeDtypeStruct((2, POLS), F32),
+            jax.ShapeDtypeStruct(dipole.shape, F32),
+        ),
+        in_specs=[pl.BlockSpec(memory_space=pltpu.VMEM)] * 3,
+        out_specs=[pl.BlockSpec(memory_space=pl.ANY)] * 3,
+        scratch_shapes=[dma((3,))],
+    )(*[pltpu.with_memory_space_constraint(r, pltpu.VMEM) for r in results])
+    return alphas.T, betas.T, last
 
 
 def solution(mesh):

time: 43.7 us -> 39.5 us (0.904)
  local copies, waits for them, and re-layouts: 4.11 us -> 0 us
    pallas_call x2 -> x0, local copies, waits for them, and re-layouts: 2.63 us -> none  [lanczos(): pl.pallas_call(functools.partial(kernel, sizes), out_shape=(jax.ShapeDtyp...]
    unnamed x1 -> x0, local copies, waits for them, and re-layouts: 1.48 us -> none
    pallas_call x1 -> x2, Pallas kernels: 38.8 us -> 38.8 us  [the longest x1 38.1 us: lanczos(): pl.pallas_call(functools.partial(kernel, sizes), out_shape=(pltpu.VMEM((2...]
where the time goes in v3:
time: 39.5 us; the launch traced here: 39.4 us
  Pallas kernels  38.8 us (98%)
  between operations  0.64 us (2%)
    pallas_call x1, Pallas kernels, lanczos(): pl.pallas_call(functools.partial(kernel, sizes), out_shape=(pltpu.VMEM((2...  38.1 us

profile of v3, /device:TPU:1, one launch (start us, length us, event | category | flops | bytes accessed | tf_op | source)
XLA Modules:
  0.0 39.4 jit_solution(14049714280879408645)
XLA Ops:
  0.6 38.1 %shard_map.76 = (f32[2,3]{1,0:T(2,128)S(1)}, f32[2,3]{1,0:T(2,128)S(1)}, f32[3,4096]{1,0:T(4,128)S(1)}) custom-call(bf16[4096,256]{1,0:T(8,128)(2,1)} %w_hbm.1, f32[3,4096]{1,0:T(4,128)} %dip_hbm.1, f32[2,512]{1,0:T(2,128)} %band_hbm.1, f32[4]{0:T(128)} %core_hbm.1, s32[8]{0:T(128)} %index_hbm.1), custom_call_target="tpu_custom_call" | custom-call | tf_op jit(solution)/shard_map/pallas_call | solution.py:502
  38.8 0.7 %shard_map.77 = (f32[2,3]{1,0:T(2,128)}, f32[2,3]{1,0:T(2,128)}, f32[3,4096]{1,0:T(4,128)}) custom-call(f32[2,3]{1,0:T(2,128)S(1)} %get-tuple-element.9.refs_0_, f32[2,3]{1,0:T(2,128)S(1)} %get-tuple-element.10.refs_1_, f32[3,4096]{1,0:T(4,128)S(1)} %get-tuple-element.11.refs_2_), custom_call_target="tpu_custom_call" | custom-call | tf_op jit(solution)/shard_map/pallas_call | solution.py:542

commit v4 on v3

--- a/solution.py
+++ b/solution.py
@@ -76,7 +76,14 @@
     def greet(d):
         pl.semaphore_signal(barrier, inc=1, device_id=d, device_id_type=MESH)
 
-    beside = [(dx, j) for dx in (2, 1, 3, 0) for j in range(4)]
+    far_first = sorted(range(1, nz), key=lambda d: -min(d, nz - d))
+
+    @pl.when(owner)
+    def _():
+        for d in far_first:
+            greet(dev(p, x, (z + d) % nz, h, 1))
+
+    beside = [(dx, j) for dx in (2, 1, 3, 0) for j in (2, 3, 1, 0)]
     for dx, j in beside:
         hh, pp = (h + j // 2) % 2, (p + j % 2) % 2
         if (dx, j) == (0, 0):
@@ -86,8 +93,6 @@
 
     @pl.when(owner)
     def _():
-        for d in sorted(range(1, nz), key=lambda d: -min(d, nz - d)):
-            greet(dev(p, x, (z + d) % nz, h, 1))
         for dx, j in beside:
             if (dx, j) != (0, 0):
                 greet(dev((p + j % 2) % 2, (x + dx) % nx, z, (h + j // 2) % 2, 0))
@@ -103,30 +108,18 @@
     big = w.shape[0] // 4
     w_loads = [
         pltpu.make_async_copy(
-            w_hbm.at[pl.ds(i * big, big)], w.at[pl.ds(i * big, big)], load_sem.at[2 + i]
+            w_hbm.at[pl.ds(i * big, big)], w.at[pl.ds(i * big, big)], load_sem.at[2]
         )
         for i in range(4)
     ]
     for c in w_loads:
         c.start()
 
-    ends = []
-
-    def start(make, condition=None, within=None):
+    def start(copy, condition=None):
         if condition is None:
-            make().start()
+            copy().start()
         else:
-            pl.when(condition)(lambda: make().start())
-        ends.append((make, condition, within))
-
-    def finish():
-        for make, condition, within in ends:
-            if condition is None and within is None:
-                make().wait_send()
-            elif condition is None or within is None:
-                pl.when(within if condition is None else condition)(lambda make=make: make().wait_send())
-            else:
-                pl.when(jnp.logical_and(condition, within))(lambda make=make: make().wait_send())
+            pl.when(condition)(lambda: copy().start())
 
     def send(src, dst, send_sem, recv_sem, device):
         return pltpu.make_async_remote_copy(
@@ -136,8 +129,43 @@
 
     me = dev(p, x, z, h, k)
 
-    def arrived(dst, recv_sem, spare_sem):
-        send(dst, dst, spare_sem, recv_sem, me).wait_recv()
+    def arrived(dst, recv_sem):
+        send(dst, dst, s1.at[0], recv_sem, me).wait_recv()
+
+    def left_here(src, send_sem):
+        send(src, src, send_sem, r1.at[0], me).wait_send()
+
+    def either(condition, then, other):
+        pl.when(condition)(then)
+        pl.when(jnp.logical_not(condition))(other)
+
+    def finish():
+        @pl.when(owner)
+        def _():
+            @pl.when(is_home)
+            def _():
+                left_here(dip.at[:, pl.ds(0, 6 * 2 * LANES)], s0.at[0])
+
+            @pl.when(keeper)
+            def _():
+                left_here(recvc.at[pl.ds(0, 6)], st.at[0])
+
+            left_here(recv2.at[pl.ds(0, 2 * (nz - 1))], s2.at[0])
+            for step in range(2):
+                left_here(recv3.at[pl.ds(0, 7)], s3.at[step])
+                left_here(recvn.at[pl.ds(0, 16 - step)], sn.at[step])
+            left_here(recvc.at[pl.ds(0, 14)], sx.at[0])
+
+        either(
+            owner,
+            lambda: left_here(recv1.at[pl.ds(0, 6)], s1.at[0]),
+            lambda: left_here(recv1.at[pl.ds(0, 8)], s1.at[0]),
+        )
+        either(
+            jnp.logical_and(owner, is_home),
+            lambda: left_here(recvc.at[pl.ds(0, 2)], sc.at[0]),
+            lambda: left_here(recvc.at[pl.ds(0, 4)], sc.at[0]),
+        )
 
     for c in loads:
         c.wait()
@@ -170,7 +198,7 @@
 
     def first_copy(dx, kk):
         return send(
-            dip.at[:, own_lines(kk)], uc0, s0.at[dx - 1, kk], r0.at[0], dev(p, (x + dx) % nx, z, h, kk)
+            dip.at[:, own_lines(kk)], uc0, s0.at[0], r0.at[0], dev(p, (x + dx) % nx, z, h, kk)
         )
 
     for dx in (2, 1, 3):
@@ -181,8 +209,7 @@
     def _():
         uc0[...] = dip[:, own_lines(k)]
 
-    for c in w_loads:
-        c.wait()
+    pltpu.make_async_copy(w_hbm, w, load_sem.at[2]).wait()
 
     row_mod = lax.broadcasted_iota(jnp.int32, (ROWS, 2 * LANES), 0) % LINES
 
@@ -202,7 +229,6 @@
 
     alpha = ratio = column = col_first = norms = None
     for step in range(2):
-        rows = ROWS + 8 if step == 0 else ROWS
         sums = jnp.zeros((ROWS, 2 * LANES), F32)
         if step == 0:
             for c in range(4):
@@ -210,25 +236,30 @@
             col_part = over_lines(sums)
             col_first = col_part
         else:
-            for jh, jp in near:
+            def chunk_share(jh, jp):
                 hh, pp = (h + jh) % 2, (p + jp) % 2
                 c = hh * 2 + pp
-                hear = functools.partial(arrived, recv3.at[0, c], r3.at[0, c], s3.at[0, 0])
+                hear = functools.partial(arrived, recv3.at[c], r3.at[c])
                 if (jh, jp) == (0, 0):
                     pl.when(jnp.logical_not(owner))(hear)
                 else:
                     hear()
-                sums += columns_of(recv3[0, c], hh, pp)
-            for xx in range(nx):
-                pl.when(jnp.logical_not(jnp.logical_and(owner, x == xx)))(
-                    functools.partial(arrived, recvx.at[0, xx], rx.at[0, xx], sx.at[0, 0])
-                )
-            whole = recvx[0, 0]
+                return columns_of(recv3[c], hh, pp)
+
+            for jh, jp in near[:3]:
+                sums += chunk_share(jh, jp)
+            either(
+                owner,
+                lambda: arrived(recvx.at[pl.ds(0, nx - 1)], rx.at[0]),
+                lambda: arrived(recvx.at[pl.ds(0, nx)], rx.at[0]),
+            )
+            whole = recvx[0]
             for xx in range(1, nx):
-                whole += recvx[0, xx]
+                whole += recvx[xx]
             whole = jnp.broadcast_to(jnp.sum(whole, axis=1, keepdims=True), (8, LANES))
             norms = [whole[q : q + 1] for q in range(POLS)]
             alpha = [whole[4 + q : 5 + q] / norms[q] for q in range(POLS)]
+            sums += chunk_share(*near[3])
             col_part = over_lines(sums)
             col_part = [col_part[q] - alpha[q][:, :1] * col_first[q] for q in range(POLS)]
         for half in range(2):
@@ -236,7 +267,7 @@
 
         def col_copy(half, step=step):
             return send(
-                sendc.at[step, half], recvc.at[step, x, k], sc.at[step, half], rc.at[step, x, k],
+                sendc.at[step, half], recvc.at[(step * nx + x) * 2 + k], sc.at[0], rc.at[step],
                 dev(half, home, z, h, 1),
             )
 
@@ -245,24 +276,23 @@
 
             @pl.when(mine)
             def _(half=half, step=step):
-                recvc[step, x, k] = sendc[step, half]
+                recvc[(step * nx + x) * 2 + k] = sendc[step, half]
 
             start(functools.partial(col_copy, half), jnp.logical_not(mine))
 
         if step == 0:
-            pl.when(away)(functools.partial(arrived, uc0, r0.at[0], s0.at[0, 0]))
+            pl.when(away)(functools.partial(arrived, uc0, r0.at[0]))
             column = [uc0[q : q + 1, :] for q in range(POLS)]
         else:
 
             @pl.when(is_home)
             def _():
                 for half in range(2):
-                    value = recv3[0, h * 2 + half]
+                    value = recv3[h * 2 + half]
                     mask = lax.broadcasted_iota(jnp.int32, (ROWS, LANES), 0) % LINES == zl * 2 + k
                     recvt[half] = placed(over_lines(jnp.where(mask, value, 0.0)))
 
-            for half in range(2):
-                pl.when(away)(functools.partial(arrived, recvt.at[half], rt.at[half], st.at[0, 0]))
+            pl.when(away)(functools.partial(arrived, recvt, rt.at[0]))
             got = jnp.concatenate([recvt[0], recvt[1]], axis=1)
             got = jnp.where(away, jnp.where(k == 1, pltpu.roll(got, 4, 0), got), got)
             column = [got[q : q + 1] - alpha[q][:, :1] * column[q] for q in range(POLS)]
@@ -274,11 +304,10 @@
             sum_rows = placed(twice)
         left = two_terms(spread(column))
 
-        def row_copy(j, step=step, rows=rows):
+        def row_copy(j, step=step):
             jh, jp = near[j]
             return send(
-                send1.at[step, j, pl.ds(0, rows)], recv1.at[step, y * 2 + k, pl.ds(0, rows)],
-                s1.at[step, j], r1.at[step, y * 2 + k], dev((p + jp) % 2, x, z, (h + jh) % 2, 1),
+                send1.at[step, j], recv1.at[step * 8 + y * 2 + k], s1.at[0], r1.at[step], dev((p + jp) % 2, x, z, (h + jh) % 2, 1),
             )
 
         for j in (3, 2, 1, 0):
@@ -294,14 +323,13 @@
                 )
                 lines = jnp.where(row_mod[:, :LANES] == t, part, lines)
             send1[step, j, :ROWS] = lines
-            if step == 0:
-                send1[step, j, ROWS:] = sum_rows
+            send1[step, j, ROWS:] = sum_rows if step == 0 else jnp.zeros((8, LANES), F32)
             start(functools.partial(row_copy, j), None if j else jnp.logical_not(owner))
 
         if step == 1:
             factor = spread(alpha)
             for c in range(4):
-                u[1, c] = recv3[0, c] - factor * u[0, c]
+                u[1, c] = recv3[c] - factor * u[0, c]
         squares = jnp.zeros((ROWS, LANES), F32)
         weighted = jnp.zeros((ROWS, LANES), F32)
         for c in range(4):
@@ -312,51 +340,43 @@
 
         def x_copy(dx, kk, at):
             return send(
-                sendx.at[at], recvx.at[at, x], sx.at[at, (dx - 1) * 2 + kk if dx else 6], rx.at[at, x],
+                sendx.at[at], recvx.at[at * nx + x], sx.at[0], rx.at[at],
                 dev(p, (x + dx) % nx, z, h, kk),
             )
 
         def share(at):
             for dx in (2, 1, 3):
                 for kk in range(2):
-                    start(functools.partial(x_copy, dx, kk, at), None, owner)
-            start(functools.partial(x_copy, 0, 0, at), None, owner)
-            recvx[at, x] = sendx[at]
+                    start(functools.partial(x_copy, dx, kk, at))
+            start(functools.partial(x_copy, 0, 0, at))
+            recvx[at * nx + x] = sendx[at]
 
         if step == 0:
             own_sums += placed(over_lines(weighted), 4)
 
         @pl.when(owner)
-        def _(step=step, rows=rows, own_sums=own_sums):
+        def _(step=step, own_sums=own_sums):
             if step == 1:
                 sendx[1] = own_sums
                 share(1)
-            recv1[step, y * 2 + k, pl.ds(0, rows)] = send1[step, 0, pl.ds(0, rows)]
-            for jh, jp in near:
-                hh, pp = (h + jh) % 2, (p + jp) % 2
-                for kk in range(2):
-                    if (jh, jp, kk) != (0, 0, 1):
-                        g = (hh * 2 + pp) * 2 + kk
-                        arrived(recv1.at[step, g, pl.ds(0, rows)], r1.at[step, g], s1.at[step, 0])
-            total = recv1[step, 0, pl.ds(0, rows)]
+            recv1[step * 8 + y * 2 + k] = send1[step, 0]
+            arrived(recv1.at[pl.ds(step * 8, 7)], r1.at[step])
+            total = recv1[step * 8]
             for g in range(1, 8):
-                total += recv1[step, g, pl.ds(0, rows)]
-            send2[step, pl.ds(0, rows)] = total
+                total += recv1[step * 8 + g]
+            send2[step] = total
 
             @pl.when(keeper)
             def _():
+                either(
+                    p == p_keep,
+                    lambda: arrived(recvc.at[pl.ds(step * 2 * nx, 2 * nx - 1)], rc.at[step]),
+                    lambda: arrived(recvc.at[pl.ds(step * 2 * nx, 2 * nx)], rc.at[step]),
+                )
                 for kk in range(2):
-                    for xx in range(nx):
-                        hear = functools.partial(
-                            arrived, recvc.at[step, xx, kk], rc.at[step, xx, kk], sc.at[step, 0]
-                        )
-                        if kk == 0:
-                            hear()
-                        else:
-                            pl.when(jnp.logical_not(jnp.logical_and(x == xx, p == p_keep)))(hear)
-                    cols = recvc[step, 0, kk]
+                    cols = recvc[step * 2 * nx + kk]
                     for xx in range(1, nx):
-                        cols += recvc[step, xx, kk]
+                        cols += recvc[(step * nx + xx) * 2 + kk]
                     for q in range(POLS):
                         at = pl.ds(LINES * q, LINES)
                         line = jnp.broadcast_to(cols[q : q + 1], (8, LANES))
@@ -364,23 +384,19 @@
 
             def z_copy(d):
                 return send(
-                    send2.at[step, pl.ds(0, rows)], recv2.at[step, z, pl.ds(0, rows)], s2.at[step, d - 1],
-                    r2.at[step, z], dev(p, x, (z + d) % nz, h, 1),
+                    send2.at[step], recv2.at[step * nz + z], s2.at[0], r2.at[step],
+                    dev(p, x, (z + d) % nz, h, 1),
                 )
 
-            for d in sorted(range(1, nz), key=lambda d: -min(d, nz - d)):
-                start(functools.partial(z_copy, d), None, owner)
-            recv2[step, z, pl.ds(0, rows)] = send2[step, pl.ds(0, rows)]
+            for d in far_first:
+                start(functools.partial(z_copy, d))
+            recv2[step * nz + z] = send2[step]
             if step == 1:
-                for dx in range(1, nx):
-                    xx = (x + dx) % nx
-                    arrived(recvx.at[1, xx], rx.at[1, xx], sx.at[1, 0])
-            for d in range(1, nz):
-                zz = (z + d) % nz
-                arrived(recv2.at[step, zz, pl.ds(0, rows)], r2.at[step, zz], s2.at[step, 0])
-            total = recv2[step, 0, pl.ds(0, rows)]
+                arrived(recvx.at[pl.ds(nx, nx - 1)], rx.at[1])
+            arrived(recv2.at[pl.ds(step * nz, nz - 1)], r2.at[step])
+            total = recv2[step * nz]
             for zz in range(1, nz):
-                total += recv2[step, zz, pl.ds(0, rows)]
+                total += recv2[step * nz + zz]
             value = total[:ROWS] + jnp.concatenate([en[y]] * POLS, axis=0) * u[step, y]
 
             if step == 0:
@@ -395,13 +411,13 @@
 
                 def tile_copy(dx, kk):
                     return send(
-                        sendt, recvt.at[p], st.at[dx - 1, kk], rt.at[p],
+                        sendt, recvt.at[p], st.at[0], rt.at[0],
                         dev(p_keep, (x + dx) % nx, z, h, kk),
                     )
 
                 for dx in (2, 1, 3):
                     for kk in range(2):
-                        start(functools.partial(tile_copy, dx, kk), keeper, owner)
+                        start(functools.partial(tile_copy, dx, kk), keeper)
             else:
                 w1 = value - spread(alpha) * u[1, y] - spread(ratio_of(1)) * u[0, y]
                 sendn[...] = placed(over_lines(w1 * w1)) + placed(over_lines(w1 * u[1, y]), 4)
@@ -409,7 +425,7 @@
                 def sums_copy(dx, j, kk):
                     jh, jp = near[j]
                     return send(
-                        sendn, recvn.at[x, y], sn.at[dx, j, kk], rn.at[x, y],
+                        sendn, recvn.at[x * 4 + y], sn.at[kk], rn.at[0],
                         dev((p + jp) % 2, (x + dx) % nx, z, (h + jh) % 2, kk),
                     )
 
@@ -417,46 +433,44 @@
                     for j in (3, 2, 1, 0):
                         for kk in range(2):
                             if (dx, j, kk) != (0, 0, 1):
-                                start(functools.partial(sums_copy, dx, j, kk), None, owner)
-                recvn[x, y] = sendn[...]
+                                start(functools.partial(sums_copy, dx, j, kk))
+                recvn[x * 4 + y] = sendn[...]
                 send3[1] = w1
 
             def chunk_copy(j, kk):
                 jh, jp = near[j]
                 return send(
-                    send3.at[step], recv3.at[step, y], s3.at[step, j * 2 + kk], r3.at[step, y],
+                    send3.at[step], recv3.at[step * 4 + y], s3.at[step], r3.at[step * 4 + y],
                     dev((p + jp) % 2, x, z, (h + jh) % 2, kk),
                 )
 
             for j in (3, 2, 1, 0):
                 for kk in range(2):
                     if (j, kk) != (0, 1):
-                        start(functools.partial(chunk_copy, j, kk), None, owner)
-            recv3[step, y] = send3[step]
+                        start(functools.partial(chunk_copy, j, kk))
+            recv3[step * 4 + y] = send3[step]
 
         def ratio_of(at):
-            whole = recvx[at, 0]
+            whole = recvx[at * nx]
             for xx in range(1, nx):
-                whole += recvx[at, xx]
+                whole += recvx[at * nx + xx]
             whole = jnp.broadcast_to(jnp.sum(whole, axis=1, keepdims=True), (8, LANES))
             return [whole[q : q + 1] / norms[q] for q in range(POLS)]
 
     @pl.when(jnp.logical_not(owner))
     def _():
-        for xx in range(nx):
-            arrived(recvx.at[1, xx], rx.at[1, xx], sx.at[1, 0])
+        arrived(recvx.at[pl.ds(nx, nx)], rx.at[1])
 
     ratio = ratio_of(1)
     norm1 = [ratio[q] * norms[q] for q in range(POLS)]
-    for xx in range(nx):
-        for c in range(4):
-            pl.when(jnp.logical_not(jnp.logical_and(owner, jnp.logical_and(x == xx, y == c))))(
-                functools.partial(arrived, recvn.at[xx, c], rn.at[xx, c], sn.at[0, 0, 0])
-            )
-    whole = jnp.zeros((8, LANES), F32)
-    for xx in range(nx):
-        for c in range(4):
-            whole += recvn[xx, c]
+    either(
+        owner,
+        lambda: arrived(recvn.at[pl.ds(0, 4 * nx - 1)], rn.at[0]),
+        lambda: arrived(recvn.at[pl.ds(0, 4 * nx)], rn.at[0]),
+    )
+    whole = recvn[0]
+    for c in range(1, 4 * nx):
+        whole += recvn[c]
     whole = jnp.broadcast_to(jnp.sum(whole, axis=1, keepdims=True), (8, LANES))
     shift = [whole[4 + q : 5 + q] / norm1[q] for q in range(POLS)]
     norm2 = [whole[q : q + 1] - shift[q] * whole[4 + q : 5 + q] for q in range(POLS)]
@@ -464,13 +478,13 @@
     back = spread(shift)
     for jh, jp in near:
         c = (h + jh) % 2 * 2 + (p + jp) % 2
-        hear = functools.partial(arrived, recv3.at[1, c], r3.at[1, c], s3.at[1, 0])
+        hear = functools.partial(arrived, recv3.at[4 + c], r3.at[4 + c])
         if (jh, jp) == (0, 0):
             pl.when(jnp.logical_not(owner))(hear)
         else:
             hear()
     for c in range(4):
-        value = (recv3[1, c] - back * u[1, c]) * inverse
+        value = (recv3[4 + c] - back * u[1, c]) * inverse
         for q in range(POLS):
             for t in range(LINES):
                 at = ((t // 2) * 8 + (c // 2) * 4 + (t % 2) * 2 + c % 2) * LANES
@@ -514,28 +528,28 @@
             pltpu.VMEM((2, 4, *chunk), F32),
             pltpu.VMEM((4, *tile), F32),
             pltpu.VMEM((2, 4, *longer), F32),
-            pltpu.VMEM((2, 8, *longer), F32),
+            pltpu.VMEM((2 * 8, *longer), F32),
             pltpu.VMEM((2, 2, *tile), F32),
-            pltpu.VMEM((2, nx, 2, *tile), F32),
+            pltpu.VMEM((2 * nx * 2, *tile), F32),
             pltpu.VMEM((2, *longer), F32),
-            pltpu.VMEM((2, nz, *longer), F32),
+            pltpu.VMEM((2 * nz, *longer), F32),
             pltpu.VMEM((2, *chunk), F32),
-            pltpu.VMEM((2, 4, *chunk), F32),
+            pltpu.VMEM((2 * 4, *chunk), F32),
             pltpu.VMEM(tile, F32),
             pltpu.VMEM((2, *tile), F32),
             pltpu.VMEM((2, *tile), F32),
-            pltpu.VMEM((2, nx, *tile), F32),
+            pltpu.VMEM((2 * nx, *tile), F32),
             pltpu.VMEM(tile, F32),
-            pltpu.VMEM((nx, 4, *tile), F32),
-            dma((6,)), dma((2,)),
-            dma((nx - 1, 2)), dma((1,)),
-            dma((2, 4)), dma((2, 8)),
-            dma((2, 2)), dma((2, nx, 2)),
-            dma((2, nz - 1)), dma((2, nz)),
-            dma((2, 8)), dma((2, 4)),
-            dma((nx - 1, 2)), dma((2,)),
-            dma((2, 7)), dma((2, nx)),
-            dma((nx, 4, 2)), dma((nx, 4)),
+            pltpu.VMEM((nx * 4, *tile), F32),
+            dma((3,)), dma((2,)),
+            dma((1,)), dma((1,)),
+            dma((1,)), dma((2,)),
+            dma((1,)), dma((2,)),
+            dma((1,)), dma((2,)),
+            dma((2,)), dma((8,)),
+            dma((1,)), dma((1,)),
+            dma((1,)), dma((2,)),
+            dma((2,)), dma((1,)),
         ],
         compiler_params=pltpu.CompilerParams(collective_id=0, has_side_effects=True),
     )(kernel_half, dipole, band_energy, core_energy, core_index)

time: 39.5 us -> 37.9 us (0.959)
  Pallas kernels: 38.8 us -> 37.2 us
    pallas_call x1, Pallas kernels: 38.1 us -> 36.5 us  [lanczos(): pl.pallas_call(functools.partial(kernel, sizes), out_shape=(pltpu.VMEM((2...]
where the time goes in v4:
time: 37.9 us; the launch traced here: 37.8 us
  Pallas kernels  37.2 us (98%)
  between operations  0.64 us (2%)
    pallas_call x1, Pallas kernels, lanczos(): pl.pallas_call(functools.partial(kernel, sizes), out_shape=(pltpu.VMEM((2...  36.5 us

profile of v4, /device:TPU:1, one launch (start us, length us, event | category | flops | bytes accessed | tf_op | source)
XLA Modules:
  0.0 37.8 jit_solution(9192214966947865147)
XLA Ops:
  0.6 36.5 %shard_map.76 = (f32[2,3]{1,0:T(2,128)S(1)}, f32[2,3]{1,0:T(2,128)S(1)}, f32[3,4096]{1,0:T(4,128)S(1)}) custom-call(bf16[4096,256]{1,0:T(8,128)(2,1)} %w_hbm.1, f32[3,4096]{1,0:T(4,128)} %dip_hbm.1, f32[2,512]{1,0:T(2,128)} %band_hbm.1, f32[4]{0:T(128)} %core_hbm.1, s32[8]{0:T(128)} %index_hbm.1), custom_call_target="tpu_custom_call" | custom-call | tf_op jit(solution)/shard_map/pallas_call | solution.py:516
  37.1 0.7 %shard_map.77 = (f32[2,3]{1,0:T(2,128)}, f32[2,3]{1,0:T(2,128)}, f32[3,4096]{1,0:T(4,128)}) custom-call(f32[2,3]{1,0:T(2,128)S(1)} %get-tuple-element.9.refs_0_, f32[2,3]{1,0:T(2,128)S(1)} %get-tuple-element.10.refs_1_, f32[3,4096]{1,0:T(4,128)S(1)} %get-tuple-element.11.refs_2_), custom_call_target="tpu_custom_call" | custom-call | tf_op jit(solution)/shard_map/pallas_call | solution.py:556

commit v5 on v4

--- a/solution.py
+++ b/solution.py
@@ -46,10 +46,10 @@
     sizes,
     w_hbm, dip_hbm, band_hbm, core_hbm, index_hbm,
     alpha_ref, beta_ref, last_ref,
-    w, dip, band, core, index,
+    w, wt, dip, band, core, index,
     uc0, u, en,
     send1, recv1, sendc, recvc, send2, recv2, send3, recv3, sendt, recvt, sendx, recvx, sendn, recvn,
-    load_sem, core_sem, s0, r0, s1, r1, sc, rc, s2, r2, s3, r3, st, rt, sx, rx, sn, rn,
+    load_sem, core_sem, s0, r0, s1, r1, sc, rc, s2, r2, s3, r3, st, rt, sx, rx, sn, rn, known, rounds,
 ):
     nx, nz, zl_count = sizes
     zh_count = nz // zl_count
@@ -72,30 +72,32 @@
         return (pp, xx, zz * 4 + hh * 2 + kk)
 
     barrier = pltpu.get_barrier_semaphore()
-
-    def greet(d):
-        pl.semaphore_signal(barrier, inc=1, device_id=d, device_id_type=MESH)
-
     far_first = sorted(range(1, nz), key=lambda d: -min(d, nz - d))
+    near = [(0, 0), (0, 1), (1, 1), (1, 0)]
+
+    def signal(sem, d):
+        pl.semaphore_signal(sem, inc=1, device_id=d, device_id_type=MESH)
+
+    def member(jh, jp, kk):
+        return dev((p + jp) % 2, x, z, (h + jh) % 2, kk)
+
+    def above_and_below(sem):
+        for d in (1, nz - 1):
+            signal(sem, dev(p, x, (z + d) % nz, h, 1))
+
+    for dx in (2, 1, 3):
+        signal(barrier, dev(p, (x + dx) % nx, z, h, 1))
+    for jh, jp in near[:0:-1]:
+        signal(barrier, member(jh, jp, 1))
+    signal(barrier, dev(p, x, z, h, 1 - k))
 
     @pl.when(owner)
     def _():
-        for d in far_first:
-            greet(dev(p, x, (z + d) % nz, h, 1))
-
-    beside = [(dx, j) for dx in (2, 1, 3, 0) for j in (2, 3, 1, 0)]
-    for dx, j in beside:
-        hh, pp = (h + j // 2) % 2, (p + j % 2) % 2
-        if (dx, j) == (0, 0):
-            greet(dev(p, x, z, h, 1 - k))
-        else:
-            greet(dev(pp, (x + dx) % nx, z, hh, 1))
-
-    @pl.when(owner)
-    def _():
-        for dx, j in beside:
-            if (dx, j) != (0, 0):
-                greet(dev((p + j % 2) % 2, (x + dx) % nx, z, (h + j // 2) % 2, 0))
+        for dx in (2, 1, 3):
+            signal(barrier, dev(p, (x + dx) % nx, z, h, 0))
+        for jh, jp in near[:0:-1]:
+            signal(barrier, member(jh, jp, 0))
+        above_and_below(barrier)
 
     loads = [
         pltpu.make_async_copy(dip_hbm, dip, load_sem.at[0]),
@@ -167,7 +169,34 @@
             lambda: left_here(recvc.at[pl.ds(0, 4)], sc.at[0]),
         )
 
-    for c in loads:
+    loads[0].wait()
+    pl.semaphore_wait(barrier, jnp.where(owner, 7 + 2 * (nx - 1) + 2, 4 + nx - 1))
+
+    @pl.when(owner)
+    def _():
+        for jh, jp in near[:0:-1]:
+            for kk in range(2):
+                signal(known, member(jh, jp, kk))
+        signal(known, dev(p, x, z, h, 0))
+        above_and_below(rounds.at[0])
+
+    def own_lines(kk):
+        return pl.ds(pl.multiple_of((zl * 4 + h * 2 + kk) * 2 * LANES, 2 * LANES), 2 * LANES)
+
+    def first_copy(dx, kk):
+        return send(
+            dip.at[:, own_lines(kk)], uc0, s0.at[0], r0.at[0], dev(p, (x + dx) % nx, z, h, kk)
+        )
+
+    for dx in (2, 1, 3):
+        for kk in range(2):
+            start(functools.partial(first_copy, dx, kk), jnp.logical_and(is_home, owner))
+
+    @pl.when(is_home)
+    def _():
+        uc0[...] = dip[:, own_lines(k)]
+
+    for c in loads[1:]:
         c.wait()
     for c in range(4):
         for q in range(POLS):
@@ -191,24 +220,6 @@
             value = jnp.where(row8 == t, jnp.broadcast_to(level, (8, LANES)), value)
         en[c] = value
 
-    pl.semaphore_wait(barrier, jnp.where(owner, 2 * len(beside) - 1 + nz - 1, len(beside)))
-
-    def own_lines(kk):
-        return pl.ds(pl.multiple_of((zl * 4 + h * 2 + kk) * 2 * LANES, 2 * LANES), 2 * LANES)
-
-    def first_copy(dx, kk):
-        return send(
-            dip.at[:, own_lines(kk)], uc0, s0.at[0], r0.at[0], dev(p, (x + dx) % nx, z, h, kk)
-        )
-
-    for dx in (2, 1, 3):
-        for kk in range(2):
-            start(functools.partial(first_copy, dx, kk), jnp.logical_and(is_home, owner))
-
-    @pl.when(is_home)
-    def _():
-        uc0[...] = dip[:, own_lines(k)]
-
     pltpu.make_async_copy(w_hbm, w, load_sem.at[2]).wait()
 
     row_mod = lax.broadcasted_iota(jnp.int32, (ROWS, 2 * LANES), 0) % LINES
@@ -225,7 +236,32 @@
             out = jnp.where(row_mod == t, part, out)
         return out
 
-    near = [(0, 0), (0, 1), (1, 1), (1, 0)]
+    def send_columns(step, col_part):
+        for half in range(2):
+            sendc[step, half] = placed([t[:, half * LANES : (half + 1) * LANES] for t in col_part])
+
+        def col_copy(half):
+            return send(
+                sendc.at[step, half], recvc.at[(step * nx + x) * 2 + k], sc.at[0], rc.at[step],
+                dev(half, home, z, h, 1),
+            )
+
+        for half in range(2):
+            mine = jnp.logical_and(owner, jnp.logical_and(is_home, p == half))
+
+            @pl.when(mine)
+            def _(half=half):
+                recvc[(step * nx + x) * 2 + k] = sendc[step, half]
+
+            start(functools.partial(col_copy, half), jnp.logical_not(mine))
+
+    def transpose():
+        side = w.shape[1]
+
+        @pl.loop(0, w.shape[0] // side)
+        def _(i):
+            at = pl.ds(pl.multiple_of(i * side, side), side)
+            wt[:, at] = w[at, :].T
 
     alpha = ratio = column = col_first = norms = None
     for step in range(2):
@@ -262,27 +298,20 @@
             sums += chunk_share(*near[3])
             col_part = over_lines(sums)
             col_part = [col_part[q] - alpha[q][:, :1] * col_first[q] for q in range(POLS)]
-        for half in range(2):
-            sendc[step, half] = placed([t[:, half * LANES : (half + 1) * LANES] for t in col_part])
-
-        def col_copy(half, step=step):
-            return send(
-                sendc.at[step, half], recvc.at[(step * nx + x) * 2 + k], sc.at[0], rc.at[step],
-                dev(half, home, z, h, 1),
-            )
-
-        for half in range(2):
-            mine = jnp.logical_and(owner, jnp.logical_and(is_home, p == half))
-
-            @pl.when(mine)
-            def _(half=half, step=step):
-                recvc[(step * nx + x) * 2 + k] = sendc[step, half]
-
-            start(functools.partial(col_copy, half), jnp.logical_not(mine))
+        if step == 1:
+            send_columns(1, col_part)
 
         if step == 0:
             pl.when(away)(functools.partial(arrived, uc0, r0.at[0]))
             column = [uc0[q : q + 1, :] for q in range(POLS)]
+            pl.semaphore_wait(known, jnp.where(owner, 3, 4))
+            send_columns(0, col_part)
+
+            @pl.when(owner)
+            def _():
+                pl.semaphore_wait(rounds.at[0], 2)
+                above_and_below(rounds.at[1])
+
         else:
 
             @pl.when(is_home)
@@ -315,12 +344,14 @@
             hh, pp = (h + jh) % 2, (p + jp) % 2
             lines = jnp.zeros((ROWS, LANES), F32)
             for t in range(LINES):
-                part = joined(
-                    lax.dot_general(
+                if step == 0:
+                    part = lax.dot_general(
                         left, w[line_rows(hh, pp, t), :], (((1,), (1,)), ((), ())),
                         preferred_element_type=F32,
                     )
-                )
+                else:
+                    part = jnp.dot(left, wt[:, line_rows(hh, pp, t)], preferred_element_type=F32)
+                part = joined(part)
                 lines = jnp.where(row_mod[:, :LANES] == t, part, lines)
             send1[step, j, :ROWS] = lines
             send1[step, j, ROWS:] = sum_rows if step == 0 else jnp.zeros((8, LANES), F32)
@@ -354,8 +385,14 @@
         if step == 0:
             own_sums += placed(over_lines(weighted), 4)
 
+        if step == 0:
+            pl.when(jnp.logical_not(owner))(transpose)
+
         @pl.when(owner)
         def _(step=step, own_sums=own_sums):
+            if step == 0:
+                pl.semaphore_wait(rounds.at[1], 2)
+                above_and_below(rounds.at[2])
             if step == 1:
                 sendx[1] = own_sums
                 share(1)
@@ -382,6 +419,8 @@
                         line = jnp.broadcast_to(cols[q : q + 1], (8, LANES))
                         send2[step, at] = send2[step, at] + jnp.where(row8 == zl * 2 + kk, line, 0.0)
 
+            if step == 0:
+                pl.semaphore_wait(rounds.at[2], 2)
             def z_copy(d):
                 return send(
                     send2.at[step], recv2.at[step * nz + z], s2.at[0], r2.at[step],
@@ -391,13 +430,17 @@
             for d in far_first:
                 start(functools.partial(z_copy, d))
             recv2[step * nz + z] = send2[step]
-            if step == 1:
+            rest = jnp.concatenate([en[y]] * POLS, axis=0) * u[step, y]
+            if step == 0:
+                transpose()
+            else:
                 arrived(recvx.at[pl.ds(nx, nx - 1)], rx.at[1])
+                rest = rest - spread(alpha) * u[1, y] - spread(ratio_of(1)) * u[0, y]
             arrived(recv2.at[pl.ds(step * nz, nz - 1)], r2.at[step])
             total = recv2[step * nz]
             for zz in range(1, nz):
                 total += recv2[step * nz + zz]
-            value = total[:ROWS] + jnp.concatenate([en[y]] * POLS, axis=0) * u[step, y]
+            value = total[:ROWS] + rest
 
             if step == 0:
                 sendx[0] = jnp.concatenate([total[ROWS + 4 :], total[ROWS : ROWS + 4]], axis=0) + own_sums
@@ -419,8 +462,7 @@
                     for kk in range(2):
                         start(functools.partial(tile_copy, dx, kk), keeper)
             else:
-                w1 = value - spread(alpha) * u[1, y] - spread(ratio_of(1)) * u[0, y]
-                sendn[...] = placed(over_lines(w1 * w1)) + placed(over_lines(w1 * u[1, y]), 4)
+                sendn[...] = placed(over_lines(value * value)) + placed(over_lines(value * u[1, y]), 4)
 
                 def sums_copy(dx, j, kk):
                     jh, jp = near[j]
@@ -435,7 +477,7 @@
                             if (dx, j, kk) != (0, 0, 1):
                                 start(functools.partial(sums_copy, dx, j, kk))
                 recvn[x * 4 + y] = sendn[...]
-                send3[1] = w1
+                send3[1] = value
 
             def chunk_copy(j, kk):
                 jh, jp = near[j]
@@ -520,6 +562,7 @@
         out_specs=[pl.BlockSpec(memory_space=pltpu.VMEM)] * 3,
         scratch_shapes=[
             pltpu.VMEM((rows, cols), BF),
+            pltpu.VMEM((cols, rows), BF),
             pltpu.VMEM(dipole.shape, F32),
             pltpu.VMEM(band_energy.shape, F32),
             pltpu.SMEM(core_energy.shape, F32),
@@ -550,6 +593,7 @@
             dma((1,)), dma((1,)),
             dma((1,)), dma((2,)),
             dma((2,)), dma((1,)),
+            pltpu.SemaphoreType.REGULAR, pltpu.SemaphoreType.REGULAR((3,)),
         ],
         compiler_params=pltpu.CompilerParams(collective_id=0, has_side_effects=True),
     )(kernel_half, dipole, band_energy, core_energy, core_index)

time: 37.9 us -> 36.8 us (0.971)
  Pallas kernels: 37.2 us -> 36 us
    pallas_call x1, Pallas kernels: 36.5 us -> 35.3 us  [lanczos(): pl.pallas_call(functools.partial(kernel, sizes), out_shape=(pltpu.VMEM((2...]
where the time goes in v5:
time: 36.8 us; the launch traced here: 36.6 us
  Pallas kernels  36 us (98%)
  between operations  0.64 us (2%)
    pallas_call x1, Pallas kernels, lanczos(): pl.pallas_call(functools.partial(kernel, sizes), out_shape=(pltpu.VMEM((2...  35.3 us

profile of v5, /device:TPU:1, one launch (start us, length us, event | category | flops | bytes accessed | tf_op | source)
XLA Modules:
  0.0 36.6 jit_solution(15147874274749580747)
XLA Ops:
  0.6 35.3 %shard_map.76 = (f32[2,3]{1,0:T(2,128)S(1)}, f32[2,3]{1,0:T(2,128)S(1)}, f32[3,4096]{1,0:T(4,128)S(1)}) custom-call(bf16[4096,256]{1,0:T(8,128)(2,1)} %w_hbm.1, f32[3,4096]{1,0:T(4,128)} %dip_hbm.1, f32[2,512]{1,0:T(2,128)} %band_hbm.1, f32[4]{0:T(128)} %core_hbm.1, s32[8]{0:T(128)} %index_hbm.1), custom_call_target="tpu_custom_call" | custom-call | tf_op jit(solution)/shard_map/pallas_call | solution.py:558
  36.0 0.7 %shard_map.77 = (f32[2,3]{1,0:T(2,128)}, f32[2,3]{1,0:T(2,128)}, f32[3,4096]{1,0:T(4,128)}) custom-call(f32[2,3]{1,0:T(2,128)S(1)} %get-tuple-element.9.refs_0_, f32[2,3]{1,0:T(2,128)S(1)} %get-tuple-element.10.refs_1_, f32[3,4096]{1,0:T(4,128)S(1)} %get-tuple-element.11.refs_2_), custom_call_target="tpu_custom_call" | custom-call | tf_op jit(solution)/shard_map/pallas_call | solution.py:600

commit v6 on v5

--- a/solution.py
+++ b/solution.py
@@ -46,10 +46,10 @@
     sizes,
     w_hbm, dip_hbm, band_hbm, core_hbm, index_hbm,
     alpha_ref, beta_ref, last_ref,
-    w, wt, dip, band, core, index,
+    w, wt, wb, wtb, colb, dip, band, core, index,
     uc0, u, en,
     send1, recv1, sendc, recvc, send2, recv2, send3, recv3, sendt, recvt, sendx, recvx, sendn, recvn,
-    load_sem, core_sem, s0, r0, s1, r1, sc, rc, s2, r2, s3, r3, st, rt, sx, rx, sn, rn, known, rounds,
+    load_sem, core_sem, s0, r0, s1, r1, sc, rc, s2, r2, s3, r3, st, rt, sx, rx, sn, rn, known, rounds, sb, rb,
 ):
     nx, nz, zl_count = sizes
     zh_count = nz // zl_count
@@ -146,11 +146,11 @@
         def _():
             @pl.when(is_home)
             def _():
-                left_here(dip.at[:, pl.ds(0, 6 * 2 * LANES)], s0.at[0])
+                left_here(dip.at[:, pl.ds(0, 6 * 4 * LANES)], s0.at[0])
 
             @pl.when(keeper)
             def _():
-                left_here(recvc.at[pl.ds(0, 6)], st.at[0])
+                left_here(recvc.at[pl.ds(0, 3)], st.at[0])
 
             left_here(recv2.at[pl.ds(0, 2 * (nz - 1))], s2.at[0])
             for step in range(2):
@@ -161,10 +161,17 @@
         either(
             owner,
             lambda: left_here(recv1.at[pl.ds(0, 6)], s1.at[0]),
-            lambda: left_here(recv1.at[pl.ds(0, 8)], s1.at[0]),
+            lambda: left_here(recv1.at[pl.ds(0, 4)], s1.at[0]),
         )
+
+        @pl.when(jnp.logical_not(owner))
+        def _():
+            left_here(w, sb.at[0])
+            left_here(wt, sb.at[1])
+            left_here(sendc.at[0], sb.at[2])
+
         either(
-            jnp.logical_and(owner, is_home),
+            jnp.logical_or(jnp.logical_not(owner), is_home),
             lambda: left_here(recvc.at[pl.ds(0, 2)], sc.at[0]),
             lambda: left_here(recvc.at[pl.ds(0, 4)], sc.at[0]),
         )
@@ -180,12 +187,11 @@
         signal(known, dev(p, x, z, h, 0))
         above_and_below(rounds.at[0])
 
-    def own_lines(kk):
-        return pl.ds(pl.multiple_of((zl * 4 + h * 2 + kk) * 2 * LANES, 2 * LANES), 2 * LANES)
+    chip_lines = pl.ds(pl.multiple_of((zl * 2 + h) * 4 * LANES, 4 * LANES), 4 * LANES)
 
     def first_copy(dx, kk):
         return send(
-            dip.at[:, own_lines(kk)], uc0, s0.at[0], r0.at[0], dev(p, (x + dx) % nx, z, h, kk)
+            dip.at[:, chip_lines], uc0, s0.at[0], r0.at[0], dev(p, (x + dx) % nx, z, h, kk)
         )
 
     for dx in (2, 1, 3):
@@ -194,7 +200,7 @@
 
     @pl.when(is_home)
     def _():
-        uc0[...] = dip[:, own_lines(k)]
+        uc0[...] = dip[:, chip_lines]
 
     for c in loads[1:]:
         c.wait()
@@ -228,22 +234,21 @@
         line = (t // 2) * 8 + hh * 4 + (t % 2) * 2 + pp
         return pl.ds(pl.multiple_of(line * LANES, LANES), LANES)
 
-    def columns_of(value, hh, pp):
-        left = two_terms(value)
+    def columns_of(left, block, hh, pp):
         out = jnp.zeros((ROWS, 2 * LANES), F32)
         for t in range(LINES):
-            part = joined(jnp.dot(left, w[line_rows(hh, pp, t), :], preferred_element_type=F32))
+            part = joined(jnp.dot(left, block[line_rows(hh, pp, t), :], preferred_element_type=F32))
             out = jnp.where(row_mod == t, part, out)
         return out
 
-    def send_columns(step, col_part):
+    def send_columns(step, tiles):
+        slot = x * 2 + k if step == 0 else 2 * nx + x
         for half in range(2):
-            sendc[step, half] = placed([t[:, half * LANES : (half + 1) * LANES] for t in col_part])
+            sendc[step, half] = tiles[half]
 
         def col_copy(half):
             return send(
-                sendc.at[step, half], recvc.at[(step * nx + x) * 2 + k], sc.at[0], rc.at[step],
-                dev(half, home, z, h, 1),
+                sendc.at[step, half], recvc.at[slot], sc.at[0], rc.at[step], dev(half, home, z, h, 1)
             )
 
         for half in range(2):
@@ -251,111 +256,160 @@
 
             @pl.when(mine)
             def _(half=half):
-                recvc[(step * nx + x) * 2 + k] = sendc[step, half]
+                recvc[slot] = sendc[step, half]
 
             start(functools.partial(col_copy, half), jnp.logical_not(mine))
 
+    def half_of(lines, half):
+        return [t[:, half * LANES : (half + 1) * LANES] for t in lines]
+
     def transpose():
-        side = w.shape[1]
-
-        @pl.loop(0, w.shape[0] // side)
+        @pl.loop(0, w.shape[0] // LANES)
         def _(i):
-            at = pl.ds(pl.multiple_of(i * side, side), side)
-            wt[:, at] = w[at, :].T
-
-    alpha = ratio = column = col_first = norms = None
+            source = pl.ds(pl.multiple_of(i * LANES, LANES), LANES)
+            target = pl.ds(pl.multiple_of((i // 8 * 2 + i // 2 % 2) * LANES, LANES), LANES)
+            wt[i // 4 % 2 * 2 + i % 2, :, target] = w[source, :].T
+
+    def first_sums():
+        whole = recvx[0]
+        for xx in range(1, nx):
+            whole += recvx[xx]
+        whole = jnp.broadcast_to(jnp.sum(whole, axis=1, keepdims=True), (8, LANES))
+        norms = [whole[q : q + 1] for q in range(POLS)]
+        return norms, [whole[4 + q : 5 + q] / norms[q] for q in range(POLS)]
+
+    def line_tile(value):
+        mod = lax.broadcasted_iota(jnp.int32, (ROWS, LANES), 0) % LINES
+        tile = jnp.zeros((8, LANES), F32)
+        for kk in range(2):
+            tile += placed(over_lines(jnp.where(mod == zl * 2 + kk, value, 0.0)), 4 * kk)
+        return tile
+
+    alpha = col_first = norms = None
     for step in range(2):
-        sums = jnp.zeros((ROWS, 2 * LANES), F32)
-        if step == 0:
+        def row_copy(j, step=step):
+            jh, jp = near[j]
+            return send(
+                send1.at[step, j], recv1.at[y * 2 + k if step == 0 else 8 + y], s1.at[0], r1.at[step],
+                member(jh, jp, 1),
+            )
+
+        def first_products():
+            sums = jnp.zeros((ROWS, 2 * LANES), F32)
             for c in range(4):
-                sums += columns_of(u[0, c], c // 2, c % 2)
+                sums += columns_of(two_terms(u[0, c]), w, c // 2, c % 2)
             col_part = over_lines(sums)
-            col_first = col_part
-        else:
-            def chunk_share(jh, jp):
-                hh, pp = (h + jh) % 2, (p + jp) % 2
-                c = hh * 2 + pp
-                hear = functools.partial(arrived, recv3.at[c], r3.at[c])
-                if (jh, jp) == (0, 0):
-                    pl.when(jnp.logical_not(owner))(hear)
-                else:
-                    hear()
-                return columns_of(recv3[c], hh, pp)
-
-            for jh, jp in near[:3]:
-                sums += chunk_share(jh, jp)
-            either(
-                owner,
-                lambda: arrived(recvx.at[pl.ds(0, nx - 1)], rx.at[0]),
-                lambda: arrived(recvx.at[pl.ds(0, nx)], rx.at[0]),
-            )
-            whole = recvx[0]
-            for xx in range(1, nx):
-                whole += recvx[xx]
-            whole = jnp.broadcast_to(jnp.sum(whole, axis=1, keepdims=True), (8, LANES))
-            norms = [whole[q : q + 1] for q in range(POLS)]
-            alpha = [whole[4 + q : 5 + q] / norms[q] for q in range(POLS)]
-            sums += chunk_share(*near[3])
-            col_part = over_lines(sums)
-            col_part = [col_part[q] - alpha[q][:, :1] * col_first[q] for q in range(POLS)]
-        if step == 1:
-            send_columns(1, col_part)
-
-        if step == 0:
+
             pl.when(away)(functools.partial(arrived, uc0, r0.at[0]))
-            column = [uc0[q : q + 1, :] for q in range(POLS)]
+            mine = pl.ds(pl.multiple_of(k * 2 * LANES, 2 * LANES), 2 * LANES)
+            column = [uc0[q : q + 1, mine] for q in range(POLS)]
             pl.semaphore_wait(known, jnp.where(owner, 3, 4))
-            send_columns(0, col_part)
+            send_columns(0, [placed(half_of(col_part, half)) for half in range(2)])
 
             @pl.when(owner)
             def _():
                 pl.semaphore_wait(rounds.at[0], 2)
                 above_and_below(rounds.at[1])
 
-        else:
-
-            @pl.when(is_home)
-            def _():
-                for half in range(2):
-                    value = recv3[h * 2 + half]
-                    mask = lax.broadcasted_iota(jnp.int32, (ROWS, LANES), 0) % LINES == zl * 2 + k
-                    recvt[half] = placed(over_lines(jnp.where(mask, value, 0.0)))
-
-            pl.when(away)(functools.partial(arrived, recvt, rt.at[0]))
-            got = jnp.concatenate([recvt[0], recvt[1]], axis=1)
-            got = jnp.where(away, jnp.where(k == 1, pltpu.roll(got, 4, 0), got), got)
-            column = [got[q : q + 1] - alpha[q][:, :1] * column[q] for q in range(POLS)]
-        if step == 0:
             twice = []
             for q in range(POLS):
                 line = 2.0 * col_part[q] * column[q]
                 twice.append(line[:, :LANES] + line[:, LANES:])
             sum_rows = placed(twice)
-        left = two_terms(spread(column))
-
-        def row_copy(j, step=step):
-            jh, jp = near[j]
-            return send(
-                send1.at[step, j], recv1.at[step * 8 + y * 2 + k], s1.at[0], r1.at[step], dev((p + jp) % 2, x, z, (h + jh) % 2, 1),
+            left = two_terms(spread(column))
+
+            for j in (3, 2, 1, 0):
+                jh, jp = near[j]
+                hh, pp = (h + jh) % 2, (p + jp) % 2
+                lines = jnp.zeros((ROWS, LANES), F32)
+                for t in range(LINES):
+                    part = joined(
+                        lax.dot_general(
+                            left, w[line_rows(hh, pp, t), :], (((1,), (1,)), ((), ())),
+                            preferred_element_type=F32,
+                        )
+                    )
+                    lines = jnp.where(row_mod[:, :LANES] == t, part, lines)
+                send1[0, j, :ROWS] = lines
+                send1[0, j, ROWS:] = sum_rows
+                start(functools.partial(row_copy, j), None if j else jnp.logical_not(owner))
+            return col_part
+
+        def chip_copy(i):
+            src, dst = ((w, wb), (wt, wtb), (sendc.at[0], colb))[i]
+            return send(src, dst, sb.at[i], rb.at[i], dev(p, x, z, h, 1))
+
+        def second_products(col_first):
+            for i, dst in enumerate((wb, wtb, colb)):
+                arrived(dst, rb.at[i])
+            sums = [jnp.zeros((ROWS, 2 * LANES), F32)] * 2
+
+            def add_chunk(jh, jp):
+                hh, pp = (h + jh) % 2, (p + jp) % 2
+                if (jh, jp) != (0, 0):
+                    arrived(recv3.at[hh * 2 + pp], r3.at[hh * 2 + pp])
+                left = two_terms(recv3[hh * 2 + pp])
+                for b, block in enumerate((wb, w)):
+                    sums[b] = sums[b] + columns_of(left, block, hh, pp)
+
+            for jh, jp in near[:3]:
+                add_chunk(jh, jp)
+            arrived(recvx.at[pl.ds(0, nx - 1)], rx.at[0])
+            _, alpha = first_sums()
+            add_chunk(*near[3])
+            before = [
+                [jnp.concatenate([colb[0, q : q + 1], colb[1, q : q + 1]], axis=1) for q in range(POLS)],
+                col_first,
+            ]
+            parts = []
+            for b in range(2):
+                part = over_lines(sums[b])
+                parts.append([part[q] - alpha[q][:, :1] * before[b][q] for q in range(POLS)])
+            send_columns(
+                1, [placed(half_of(parts[0], half)) + placed(half_of(parts[1], half), 4) for half in range(2)]
             )
 
-        for j in (3, 2, 1, 0):
-            jh, jp = near[j]
-            hh, pp = (h + jh) % 2, (p + jp) % 2
-            lines = jnp.zeros((ROWS, LANES), F32)
-            for t in range(LINES):
-                if step == 0:
-                    part = lax.dot_general(
-                        left, w[line_rows(hh, pp, t), :], (((1,), (1,)), ((), ())),
-                        preferred_element_type=F32,
-                    )
-                else:
-                    part = jnp.dot(left, wt[:, line_rows(hh, pp, t)], preferred_element_type=F32)
-                part = joined(part)
-                lines = jnp.where(row_mod[:, :LANES] == t, part, lines)
-            send1[step, j, :ROWS] = lines
-            send1[step, j, ROWS:] = sum_rows if step == 0 else jnp.zeros((8, LANES), F32)
-            start(functools.partial(row_copy, j), None if j else jnp.logical_not(owner))
+            @pl.when(is_home)
+            def _():
+                for half in range(2):
+                    recvt[half] = line_tile(recv3[h * 2 + half])
+
+            pl.when(away)(functools.partial(arrived, recvt, rt.at[0]))
+            lefts = []
+            for b in range(2):
+                mine = slice(b * 2 * LANES, (b + 1) * 2 * LANES)
+                column = []
+                for q in range(POLS):
+                    at = slice(4 * b + q, 4 * b + q + 1)
+                    got = jnp.concatenate([recvt[0, at], recvt[1, at]], axis=1)
+                    column.append(got - alpha[q][:, :1] * uc0[q : q + 1, mine])
+                lefts.append(two_terms(spread(column)))
+            for j in (3, 2, 1, 0):
+                jh, jp = near[j]
+                c = (h + jh) % 2 * 2 + (p + jp) % 2
+                wide = joined(
+                    jnp.dot(lefts[0], wtb[c], preferred_element_type=F32)
+                    + jnp.dot(lefts[1], wt[c], preferred_element_type=F32)
+                )
+                lines = jnp.zeros((ROWS, LANES), F32)
+                for t in range(LINES):
+                    lines = jnp.where(row_mod[:, :LANES] == t, wide[:, t * LANES : (t + 1) * LANES], lines)
+                send1[1, j, :ROWS] = lines
+                send1[1, j, ROWS:] = jnp.zeros((8, LANES), F32)
+                if j:
+                    start(functools.partial(row_copy, j))
+
+        if step == 0:
+            col_first = first_products()
+        else:
+
+            def only_wait():
+                for c in range(4):
+                    arrived(recv3.at[c], r3.at[c])
+                arrived(recvx.at[pl.ds(0, nx)], rx.at[0])
+
+            either(owner, lambda: second_products(col_first), only_wait)
+            norms, alpha = first_sums()
 
         if step == 1:
             factor = spread(alpha)
@@ -386,7 +440,13 @@
             own_sums += placed(over_lines(weighted), 4)
 
         if step == 0:
-            pl.when(jnp.logical_not(owner))(transpose)
+
+            @pl.when(jnp.logical_not(owner))
+            def _():
+                chip_copy(2).start()
+                chip_copy(0).start()
+                transpose()
+                chip_copy(1).start()
 
         @pl.when(owner)
         def _(step=step, own_sums=own_sums):
@@ -396,27 +456,31 @@
             if step == 1:
                 sendx[1] = own_sums
                 share(1)
-            recv1[step * 8 + y * 2 + k] = send1[step, 0]
-            arrived(recv1.at[pl.ds(step * 8, 7)], r1.at[step])
+            recv1[y * 2 + k if step == 0 else 8 + y] = send1[step, 0]
+            members = 4 if step else 8
+            arrived(recv1.at[pl.ds(step * 8, members - 1)], r1.at[step])
             total = recv1[step * 8]
-            for g in range(1, 8):
+            for g in range(1, members):
                 total += recv1[step * 8 + g]
             send2[step] = total
 
             @pl.when(keeper)
             def _():
+                base, many = (0, 2 * nx) if step == 0 else (2 * nx, nx)
                 either(
                     p == p_keep,
-                    lambda: arrived(recvc.at[pl.ds(step * 2 * nx, 2 * nx - 1)], rc.at[step]),
-                    lambda: arrived(recvc.at[pl.ds(step * 2 * nx, 2 * nx)], rc.at[step]),
+                    lambda: arrived(recvc.at[pl.ds(base, many - 1)], rc.at[step]),
+                    lambda: arrived(recvc.at[pl.ds(base, many)], rc.at[step]),
                 )
                 for kk in range(2):
-                    cols = recvc[step * 2 * nx + kk]
-                    for xx in range(1, nx):
-                        cols += recvc[(step * nx + xx) * 2 + kk]
+                    slots = [base + 2 * xx + kk if step == 0 else base + xx for xx in range(nx)]
+                    cols = recvc[slots[0]]
+                    for slot in slots[1:]:
+                        cols += recvc[slot]
+                    first = 0 if step == 0 else 4 * kk
                     for q in range(POLS):
                         at = pl.ds(LINES * q, LINES)
-                        line = jnp.broadcast_to(cols[q : q + 1], (8, LANES))
+                        line = jnp.broadcast_to(cols[first + q : first + q + 1], (8, LANES))
                         send2[step, at] = send2[step, at] + jnp.where(row8 == zl * 2 + kk, line, 0.0)
 
             if step == 0:
@@ -446,21 +510,15 @@
                 sendx[0] = jnp.concatenate([total[ROWS + 4 :], total[ROWS : ROWS + 4]], axis=0) + own_sums
                 share(0)
                 send3[0] = value
-                mod = lax.broadcasted_iota(jnp.int32, (ROWS, LANES), 0) % LINES
-                tile = jnp.zeros((8, LANES), F32)
-                for kk in range(2):
-                    tile += placed(over_lines(jnp.where(mod == zl * 2 + kk, value, 0.0)), 4 * kk)
-                sendt[...] = tile
-
-                def tile_copy(dx, kk):
+                sendt[...] = line_tile(value)
+
+                def tile_copy(dx):
                     return send(
-                        sendt, recvt.at[p], st.at[0], rt.at[0],
-                        dev(p_keep, (x + dx) % nx, z, h, kk),
+                        sendt, recvt.at[p], st.at[0], rt.at[0], dev(p_keep, (x + dx) % nx, z, h, 1)
                     )
 
                 for dx in (2, 1, 3):
-                    for kk in range(2):
-                        start(functools.partial(tile_copy, dx, kk), keeper)
+                    start(functools.partial(tile_copy, dx), keeper)
             else:
                 sendn[...] = placed(over_lines(value * value)) + placed(over_lines(value * u[1, y]), 4)
 
@@ -562,12 +620,15 @@
         out_specs=[pl.BlockSpec(memory_space=pltpu.VMEM)] * 3,
         scratch_shapes=[
             pltpu.VMEM((rows, cols), BF),
-            pltpu.VMEM((cols, rows), BF),
+            pltpu.VMEM((4, cols, LINES * LANES), BF),
+            pltpu.VMEM((rows, cols), BF),
+            pltpu.VMEM((4, cols, LINES * LANES), BF),
+            pltpu.VMEM((2, *tile), F32),
             pltpu.VMEM(dipole.shape, F32),
             pltpu.VMEM(band_energy.shape, F32),
             pltpu.SMEM(core_energy.shape, F32),
             pltpu.SMEM(core_index.shape, jnp.int32),
-            pltpu.VMEM((POLS, cols), F32),
+            pltpu.VMEM((POLS, 2 * cols), F32),
             pltpu.VMEM((2, 4, *chunk), F32),
             pltpu.VMEM((4, *tile), F32),
             pltpu.VMEM((2, 4, *longer), F32),
@@ -594,6 +655,7 @@
             dma((1,)), dma((2,)),
             dma((2,)), dma((1,)),
             pltpu.SemaphoreType.REGULAR, pltpu.SemaphoreType.REGULAR((3,)),
+            dma((3,)), dma((3,)),
         ],
         compiler_params=pltpu.CompilerParams(collective_id=0, has_side_effects=True),
     )(kernel_half, dipole, band_energy, core_energy, core_index)

time: 36.8 us -> 36.3 us (0.986)
  Pallas kernels: 36 us -> 35.5 us
    pallas_call x1, Pallas kernels: 35.3 us -> 34.9 us  [lanczos(): pl.pallas_call(functools.partial(kernel, sizes), out_shape=(pltpu.VMEM((2...]
where the time goes in v6:
time: 36.3 us; the launch traced here: 36.2 us
  Pallas kernels  35.5 us (98%)
  between operations  0.64 us (2%)
    pallas_call x1, Pallas kernels, lanczos(): pl.pallas_call(functools.partial(kernel, sizes), out_shape=(pltpu.VMEM((2...  34.9 us

profile of v6, /device:TPU:1, one launch (start us, length us, event | category | flops | bytes accessed | tf_op | source)
XLA Modules:
  0.0 36.2 jit_solution(6075356892540881622)
XLA Ops:
  0.6 34.9 %shard_map.76 = (f32[2,3]{1,0:T(2,128)S(1)}, f32[2,3]{1,0:T(2,128)S(1)}, f32[3,4096]{1,0:T(4,128)S(1)}) custom-call(bf16[4096,256]{1,0:T(8,128)(2,1)} %w_hbm.1, f32[3,4096]{1,0:T(4,128)} %dip_hbm.1, f32[2,512]{1,0:T(2,128)} %band_hbm.1, f32[4]{0:T(128)} %core_hbm.1, s32[8]{0:T(128)} %index_hbm.1), custom_call_target="tpu_custom_call" | custom-call | tf_op jit(solution)/shard_map/pallas_call | solution.py:616
  35.5 0.7 %shard_map.77 = (f32[2,3]{1,0:T(2,128)}, f32[2,3]{1,0:T(2,128)}, f32[3,4096]{1,0:T(4,128)}) custom-call(f32[2,3]{1,0:T(2,128)S(1)} %get-tuple-element.9.refs_0_, f32[2,3]{1,0:T(2,128)S(1)} %get-tuple-element.10.refs_1_, f32[3,4096]{1,0:T(4,128)S(1)} %get-tuple-element.11.refs_2_), custom_call_target="tpu_custom_call" | custom-call | tf_op jit(solution)/shard_map/pallas_call | solution.py:662

commit v7 on v6

--- a/solution.py
+++ b/solution.py
@@ -33,20 +33,32 @@
     return out
 
 
+def stacked(parts):
+    width = parts[0].shape[1]
+    row = lax.broadcasted_iota(jnp.int32, (8, width), 0)
+    a, b, c = (jnp.broadcast_to(t, (8, width)) for t in parts)
+    return jnp.where(row == 0, a, jnp.where(row == 1, b, c))
+
+
+def other_rows(x):
+    return jnp.concatenate([x[4:], x[:4]], axis=0)
+
+
 def two_terms(x):
     high = x.astype(BF).astype(F32)
     return jnp.concatenate([high, x - high], axis=0).astype(BF)
 
 
 def joined(x):
-    return x[:ROWS] + x[ROWS:]
+    half = x.shape[0] // 2
+    return x[:half] + x[half:]
 
 
 def kernel(
     sizes,
     w_hbm, dip_hbm, band_hbm, core_hbm, index_hbm,
     alpha_ref, beta_ref, last_ref,
-    w, wt, wb, wtb, colb, dip, band, core, index,
+    w, wt, wb, wtb, turn, dip, band, core, index,
     uc0, u, en,
     send1, recv1, sendc, recvc, send2, recv2, send3, recv3, sendt, recvt, sendx, recvx, sendn, recvn,
     load_sem, core_sem, s0, r0, s1, r1, sc, rc, s2, r2, s3, r3, st, rt, sx, rx, sn, rn, known, rounds, sb, rb,
@@ -168,7 +180,6 @@
         def _():
             left_here(w, sb.at[0])
             left_here(wt, sb.at[1])
-            left_here(sendc.at[0], sb.at[2])
 
         either(
             jnp.logical_or(jnp.logical_not(owner), is_home),
@@ -228,7 +239,9 @@
 
     pltpu.make_async_copy(w_hbm, w, load_sem.at[2]).wait()
 
-    row_mod = lax.broadcasted_iota(jnp.int32, (ROWS, 2 * LANES), 0) % LINES
+    line_of_row_wide = lax.broadcasted_iota(jnp.int32, (ROWS, 2 * LANES), 0) % LINES
+    line_of_row = lax.broadcasted_iota(jnp.int32, (ROWS, LANES), 0) % LINES
+    row8_wide = lax.broadcasted_iota(jnp.int32, (8, 2 * LANES), 0)
 
     def line_rows(hh, pp, t):
         line = (t // 2) * 8 + hh * 4 + (t % 2) * 2 + pp
@@ -238,7 +251,7 @@
         out = jnp.zeros((ROWS, 2 * LANES), F32)
         for t in range(LINES):
             part = joined(jnp.dot(left, block[line_rows(hh, pp, t), :], preferred_element_type=F32))
-            out = jnp.where(row_mod == t, part, out)
+            out = jnp.where(line_of_row_wide == t, part, out)
         return out
 
     def send_columns(step, tiles):
@@ -260,21 +273,24 @@
 
             start(functools.partial(col_copy, half), jnp.logical_not(mine))
 
-    def half_of(lines, half):
-        return [t[:, half * LANES : (half + 1) * LANES] for t in lines]
-
     def transpose():
-        @pl.loop(0, w.shape[0] // LANES)
+        side = 2 * LANES
+
+        @pl.loop(0, w.shape[0] // side)
         def _(i):
-            source = pl.ds(pl.multiple_of(i * LANES, LANES), LANES)
-            target = pl.ds(pl.multiple_of((i // 8 * 2 + i // 2 % 2) * LANES, LANES), LANES)
-            wt[i // 4 % 2 * 2 + i % 2, :, target] = w[source, :].T
-
-    def first_sums():
+            tile = w[pl.ds(pl.multiple_of(i * side, side), side), :].T
+            at = pl.ds(pl.multiple_of((i // 4 * 2 + i % 2) * LANES, LANES), LANES)
+            for pp in range(2):
+                wt[i // 2 % 2 * 2 + pp, :, at] = tile[:, pp * LANES : (pp + 1) * LANES]
+
+    def plane_sums():
         whole = recvx[0]
         for xx in range(1, nx):
             whole += recvx[xx]
-        whole = jnp.broadcast_to(jnp.sum(whole, axis=1, keepdims=True), (8, LANES))
+        return jnp.broadcast_to(jnp.sum(whole, axis=1, keepdims=True), (8, LANES))
+
+    def first_sums():
+        whole = plane_sums()
         norms = [whole[q : q + 1] for q in range(POLS)]
         return norms, [whole[4 + q : 5 + q] / norms[q] for q in range(POLS)]
 
@@ -285,7 +301,7 @@
             tile += placed(over_lines(jnp.where(mod == zl * 2 + kk, value, 0.0)), 4 * kk)
         return tile
 
-    alpha = col_first = norms = None
+    alpha = norms = None
     for step in range(2):
         def row_copy(j, step=step):
             jh, jp = near[j]
@@ -298,13 +314,14 @@
             sums = jnp.zeros((ROWS, 2 * LANES), F32)
             for c in range(4):
                 sums += columns_of(two_terms(u[0, c]), w, c // 2, c % 2)
-            col_part = over_lines(sums)
+            col_lines = over_lines(sums)
+            col_part = stacked(col_lines)
 
             pl.when(away)(functools.partial(arrived, uc0, r0.at[0]))
             mine = pl.ds(pl.multiple_of(k * 2 * LANES, 2 * LANES), 2 * LANES)
             column = [uc0[q : q + 1, mine] for q in range(POLS)]
             pl.semaphore_wait(known, jnp.where(owner, 3, 4))
-            send_columns(0, [placed(half_of(col_part, half)) for half in range(2)])
+            send_columns(0, [col_part[:, :LANES], col_part[:, LANES:]])
 
             @pl.when(owner)
             def _():
@@ -313,7 +330,7 @@
 
             twice = []
             for q in range(POLS):
-                line = 2.0 * col_part[q] * column[q]
+                line = 2.0 * col_lines[q] * column[q]
                 twice.append(line[:, :LANES] + line[:, LANES:])
             sum_rows = placed(twice)
             left = two_terms(spread(column))
@@ -329,45 +346,28 @@
                             preferred_element_type=F32,
                         )
                     )
-                    lines = jnp.where(row_mod[:, :LANES] == t, part, lines)
+                    lines = jnp.where(line_of_row == t, part, lines)
                 send1[0, j, :ROWS] = lines
                 send1[0, j, ROWS:] = sum_rows
                 start(functools.partial(row_copy, j), None if j else jnp.logical_not(owner))
-            return col_part
 
         def chip_copy(i):
-            src, dst = ((w, wb), (wt, wtb), (sendc.at[0], colb))[i]
+            src, dst = ((w, wb), (wt, wtb))[i]
             return send(src, dst, sb.at[i], rb.at[i], dev(p, x, z, h, 1))
 
-        def second_products(col_first):
-            for i, dst in enumerate((wb, wtb, colb)):
-                arrived(dst, rb.at[i])
+        def second_products():
+            arrived(wb, rb.at[0])
             sums = [jnp.zeros((ROWS, 2 * LANES), F32)] * 2
-
-            def add_chunk(jh, jp):
+            for jh, jp in near:
                 hh, pp = (h + jh) % 2, (p + jp) % 2
                 if (jh, jp) != (0, 0):
                     arrived(recv3.at[hh * 2 + pp], r3.at[hh * 2 + pp])
                 left = two_terms(recv3[hh * 2 + pp])
                 for b, block in enumerate((wb, w)):
                     sums[b] = sums[b] + columns_of(left, block, hh, pp)
-
-            for jh, jp in near[:3]:
-                add_chunk(jh, jp)
-            arrived(recvx.at[pl.ds(0, nx - 1)], rx.at[0])
-            _, alpha = first_sums()
-            add_chunk(*near[3])
-            before = [
-                [jnp.concatenate([colb[0, q : q + 1], colb[1, q : q + 1]], axis=1) for q in range(POLS)],
-                col_first,
-            ]
-            parts = []
-            for b in range(2):
-                part = over_lines(sums[b])
-                parts.append([part[q] - alpha[q][:, :1] * before[b][q] for q in range(POLS)])
-            send_columns(
-                1, [placed(half_of(parts[0], half)) + placed(half_of(parts[1], half), 4) for half in range(2)]
-            )
+            parts = [stacked(over_lines(sums[b])) for b in range(2)]
+            tiles = jnp.where(row8_wide < 4, parts[0], other_rows(parts[1]))
+            send_columns(1, [tiles[:, :LANES], tiles[:, LANES:]])
 
             @pl.when(is_home)
             def _():
@@ -375,15 +375,9 @@
                     recvt[half] = line_tile(recv3[h * 2 + half])
 
             pl.when(away)(functools.partial(arrived, recvt, rt.at[0]))
-            lefts = []
-            for b in range(2):
-                mine = slice(b * 2 * LANES, (b + 1) * 2 * LANES)
-                column = []
-                for q in range(POLS):
-                    at = slice(4 * b + q, 4 * b + q + 1)
-                    got = jnp.concatenate([recvt[0, at], recvt[1, at]], axis=1)
-                    column.append(got - alpha[q][:, :1] * uc0[q : q + 1, mine])
-                lefts.append(two_terms(spread(column)))
+            got = jnp.concatenate([recvt[0], recvt[1]], axis=1)
+            lefts = [two_terms(got), two_terms(other_rows(got))]
+            arrived(wtb, rb.at[1])
             for j in (3, 2, 1, 0):
                 jh, jp = near[j]
                 c = (h + jh) % 2 * 2 + (p + jp) % 2
@@ -391,16 +385,17 @@
                     jnp.dot(lefts[0], wtb[c], preferred_element_type=F32)
                     + jnp.dot(lefts[1], wt[c], preferred_element_type=F32)
                 )
-                lines = jnp.zeros((ROWS, LANES), F32)
                 for t in range(LINES):
-                    lines = jnp.where(row_mod[:, :LANES] == t, wide[:, t * LANES : (t + 1) * LANES], lines)
-                send1[1, j, :ROWS] = lines
+                    turn[j, 8 * t : 8 * t + 8, :] = wide[:, t * LANES : (t + 1) * LANES]
+                for q in range(POLS):
+                    send1[1, j, LINES * q : LINES * (q + 1)] = turn[j, pl.ds(q, LINES, stride=8), :]
                 send1[1, j, ROWS:] = jnp.zeros((8, LANES), F32)
                 if j:
                     start(functools.partial(row_copy, j))
+            arrived(recvx.at[pl.ds(0, nx - 1)], rx.at[0])
 
         if step == 0:
-            col_first = first_products()
+            first_products()
         else:
 
             def only_wait():
@@ -408,7 +403,7 @@
                     arrived(recv3.at[c], r3.at[c])
                 arrived(recvx.at[pl.ds(0, nx)], rx.at[0])
 
-            either(owner, lambda: second_products(col_first), only_wait)
+            either(owner, second_products, only_wait)
             norms, alpha = first_sums()
 
         if step == 1:
@@ -429,12 +424,13 @@
                 dev(p, (x + dx) % nx, z, h, kk),
             )
 
-        def share(at):
+        def share(at, kk):
             for dx in (2, 1, 3):
-                for kk in range(2):
-                    start(functools.partial(x_copy, dx, kk, at))
-            start(functools.partial(x_copy, 0, 0, at))
-            recvx[at * nx + x] = sendx[at]
+                start(functools.partial(x_copy, dx, kk, at))
+            if kk == 0:
+                start(functools.partial(x_copy, 0, 0, at))
+            else:
+                recvx[at * nx + x] = sendx[at]
 
         if step == 0:
             own_sums += placed(over_lines(weighted), 4)
@@ -443,7 +439,6 @@
 
             @pl.when(jnp.logical_not(owner))
             def _():
-                chip_copy(2).start()
                 chip_copy(0).start()
                 transpose()
                 chip_copy(1).start()
@@ -455,7 +450,8 @@
                 above_and_below(rounds.at[2])
             if step == 1:
                 sendx[1] = own_sums
-                share(1)
+                share(1, 1)
+                share(1, 0)
             recv1[y * 2 + k if step == 0 else 8 + y] = send1[step, 0]
             members = 4 if step else 8
             arrived(recv1.at[pl.ds(step * 8, members - 1)], r1.at[step])
@@ -499,17 +495,27 @@
                 transpose()
             else:
                 arrived(recvx.at[pl.ds(nx, nx - 1)], rx.at[1])
-                rest = rest - spread(alpha) * u[1, y] - spread(ratio_of(1)) * u[0, y]
+                coupled = send3[0] - jnp.concatenate([en[y]] * POLS, axis=0) * u[0, y]
+                rest = rest - spread(alpha) * (u[1, y] + coupled) - spread(ratio_of(1)) * u[0, y]
             arrived(recv2.at[pl.ds(step * nz, nz - 1)], r2.at[step])
             total = recv2[step * nz]
             for zz in range(1, nz):
                 total += recv2[step * nz + zz]
             value = total[:ROWS] + rest
 
+            def chunk_copy(j, kk):
+                jh, jp = near[j]
+                return send(
+                    send3.at[step], recv3.at[step * 4 + y], s3.at[step], r3.at[step * 4 + y],
+                    dev((p + jp) % 2, x, z, (h + jh) % 2, kk),
+                )
+
+            def send_chunk(j, kk):
+                start(functools.partial(chunk_copy, j, kk))
+
             if step == 0:
-                sendx[0] = jnp.concatenate([total[ROWS + 4 :], total[ROWS : ROWS + 4]], axis=0) + own_sums
-                share(0)
                 send3[0] = value
+                send_chunk(3, 1)
                 sendt[...] = line_tile(value)
 
                 def tile_copy(dx):
@@ -519,6 +525,13 @@
 
                 for dx in (2, 1, 3):
                     start(functools.partial(tile_copy, dx), keeper)
+                send_chunk(2, 1)
+                send_chunk(1, 1)
+                sendx[0] = jnp.concatenate([total[ROWS + 4 :], total[ROWS : ROWS + 4]], axis=0) + own_sums
+                share(0, 1)
+                for j in (3, 2, 1, 0):
+                    send_chunk(j, 0)
+                share(0, 0)
             else:
                 sendn[...] = placed(over_lines(value * value)) + placed(over_lines(value * u[1, y]), 4)
 
@@ -537,17 +550,11 @@
                 recvn[x * 4 + y] = sendn[...]
                 send3[1] = value
 
-            def chunk_copy(j, kk):
-                jh, jp = near[j]
-                return send(
-                    send3.at[step], recv3.at[step * 4 + y], s3.at[step], r3.at[step * 4 + y],
-                    dev((p + jp) % 2, x, z, (h + jh) % 2, kk),
-                )
-
-            for j in (3, 2, 1, 0):
-                for kk in range(2):
-                    if (j, kk) != (0, 1):
-                        start(functools.partial(chunk_copy, j, kk))
+            if step == 1:
+                for j in (3, 2, 1, 0):
+                    send_chunk(j, 0)
+                    if j:
+                        send_chunk(j, 1)
             recv3[step * 4 + y] = send3[step]
 
         def ratio_of(at):
@@ -623,7 +630,7 @@
             pltpu.VMEM((4, cols, LINES * LANES), BF),
             pltpu.VMEM((rows, cols), BF),
             pltpu.VMEM((4, cols, LINES * LANES), BF),
-            pltpu.VMEM((2, *tile), F32),
+            pltpu.VMEM((4, 8 * LINES, LANES), F32),
             pltpu.VMEM(dipole.shape, F32),
             pltpu.VMEM(band_energy.shape, F32),
             pltpu.SMEM(core_energy.shape, F32),
@@ -655,7 +662,7 @@
             dma((1,)), dma((2,)),
             dma((2,)), dma((1,)),
             pltpu.SemaphoreType.REGULAR, pltpu.SemaphoreType.REGULAR((3,)),
-            dma((3,)), dma((3,)),
+            dma((2,)), dma((2,)),
         ],
         compiler_params=pltpu.CompilerParams(collective_id=0, has_side_effects=True),
     )(kernel_half, dipole, band_energy, core_energy, core_index)

time: 36.3 us -> 36 us (level)
  no operation moved by 1% of the time
where the time goes in v7:
time: 36 us; the launch traced here: 35.9 us
  Pallas kernels  35.3 us (98%)
  between operations  0.64 us (2%)
    pallas_call x1, Pallas kernels, lanczos(): pl.pallas_call(functools.partial(kernel, sizes), out_shape=(pltpu.VMEM((2...  34.6 us

profile of v7, /device:TPU:1, one launch (start us, length us, event | category | flops | bytes accessed | tf_op | source)
XLA Modules:
  0.0 35.9 jit_solution(11879331771095500403)
XLA Ops:
  0.6 34.6 %shard_map.76 = (f32[2,3]{1,0:T(2,128)S(1)}, f32[2,3]{1,0:T(2,128)S(1)}, f32[3,4096]{1,0:T(4,128)S(1)}) custom-call(bf16[4096,256]{1,0:T(8,128)(2,1)} %w_hbm.1, f32[3,4096]{1,0:T(4,128)} %dip_hbm.1, f32[2,512]{1,0:T(2,128)} %band_hbm.1, f32[4]{0:T(128)} %core_hbm.1, s32[8]{0:T(128)} %index_hbm.1), custom_call_target="tpu_custom_call" | custom-call | tf_op jit(solution)/shard_map/pallas_call | solution.py:623
  35.2 0.7 %shard_map.77 = (f32[2,3]{1,0:T(2,128)}, f32[2,3]{1,0:T(2,128)}, f32[3,4096]{1,0:T(4,128)}) custom-call(f32[2,3]{1,0:T(2,128)S(1)} %get-tuple-element.9.refs_0_, f32[2,3]{1,0:T(2,128)S(1)} %get-tuple-element.10.refs_1_, f32[3,4096]{1,0:T(4,128)S(1)} %get-tuple-element.11.refs_2_), custom_call_target="tpu_custom_call" | custom-call | tf_op jit(solution)/shard_map/pallas_call | solution.py:669

commit v8 on v7

--- a/solution.py
+++ b/solution.py
@@ -58,10 +58,10 @@
     sizes,
     w_hbm, dip_hbm, band_hbm, core_hbm, index_hbm,
     alpha_ref, beta_ref, last_ref,
-    w, wt, wb, wtb, turn, dip, band, core, index,
+    w, wt, wb, wtb, turn, recvd, dip, band, core, index,
     uc0, u, en,
     send1, recv1, sendc, recvc, send2, recv2, send3, recv3, sendt, recvt, sendx, recvx, sendn, recvn,
-    load_sem, core_sem, s0, r0, s1, r1, sc, rc, s2, r2, s3, r3, st, rt, sx, rx, sn, rn, known, rounds, sb, rb,
+    load_sem, core_sem, s0, r0, s1, r1, sc, rc, s2, r2, s3, r3, st, rt, sx, rx, sn, rn, known, rounds, sb, rb, sd, rd,
 ):
     nx, nz, zl_count = sizes
     zh_count = nz // zl_count
@@ -181,11 +181,14 @@
             left_here(w, sb.at[0])
             left_here(wt, sb.at[1])
 
+        mine = jnp.logical_and(owner, is_home)
         either(
-            jnp.logical_or(jnp.logical_not(owner), is_home),
+            mine,
+            lambda: left_here(recvc.at[pl.ds(0, 1)], sc.at[0]),
             lambda: left_here(recvc.at[pl.ds(0, 2)], sc.at[0]),
-            lambda: left_here(recvc.at[pl.ds(0, 4)], sc.at[0]),
         )
+        pl.when(mine)(lambda: left_here(recvd.at[pl.ds(0, 2 * nz - 1)], sd.at[0]))
+        pl.when(jnp.logical_and(owner, away))(lambda: left_here(recvd.at[pl.ds(0, 2 * nz)], sd.at[0]))
 
     loads[0].wait()
     pl.semaphore_wait(barrier, jnp.where(owner, 7 + 2 * (nx - 1) + 2, 4 + nx - 1))
@@ -255,7 +258,7 @@
         return out
 
     def send_columns(step, tiles):
-        slot = x * 2 + k if step == 0 else 2 * nx + x
+        slot = x * 2 + k
         for half in range(2):
             sendc[step, half] = tiles[half]
 
@@ -367,7 +370,8 @@
                     sums[b] = sums[b] + columns_of(left, block, hh, pp)
             parts = [stacked(over_lines(sums[b])) for b in range(2)]
             tiles = jnp.where(row8_wide < 4, parts[0], other_rows(parts[1]))
-            send_columns(1, [tiles[:, :LANES], tiles[:, LANES:]])
+            for half in range(2):
+                sendc[1, half] = tiles[:, half * LANES : (half + 1) * LANES]
 
             @pl.when(is_home)
             def _():
@@ -377,6 +381,27 @@
             pl.when(away)(functools.partial(arrived, recvt, rt.at[0]))
             got = jnp.concatenate([recvt[0], recvt[1]], axis=1)
             lefts = [two_terms(got), two_terms(other_rows(got))]
+
+            def direct_copy(d, half):
+                return send(
+                    sendc.at[1, half], recvd.at[x * zl_count + zl], sd.at[0], rd.at[0],
+                    dev(half, home, (z + d) % nz, h, 1),
+                )
+
+            def send_direct():
+                for d in (*far_first, 0):
+                    for half in range(2):
+                        if d:
+                            start(functools.partial(direct_copy, d, half))
+                        else:
+                            mine = jnp.logical_and(is_home, p == half)
+
+                            @pl.when(mine)
+                            def _(half=half):
+                                recvd[x * zl_count + zl] = sendc[1, half]
+
+                            start(functools.partial(direct_copy, d, half), jnp.logical_not(mine))
+
             arrived(wtb, rb.at[1])
             for j in (3, 2, 1, 0):
                 jh, jp = near[j]
@@ -392,6 +417,8 @@
                 send1[1, j, ROWS:] = jnp.zeros((8, LANES), F32)
                 if j:
                     start(functools.partial(row_copy, j))
+                if j == 1:
+                    send_direct()
             arrived(recvx.at[pl.ds(0, nx - 1)], rx.at[0])
 
         if step == 0:
@@ -460,24 +487,23 @@
                 total += recv1[step * 8 + g]
             send2[step] = total
 
-            @pl.when(keeper)
-            def _():
-                base, many = (0, 2 * nx) if step == 0 else (2 * nx, nx)
+            def add_columns():
                 either(
                     p == p_keep,
-                    lambda: arrived(recvc.at[pl.ds(base, many - 1)], rc.at[step]),
-                    lambda: arrived(recvc.at[pl.ds(base, many)], rc.at[step]),
+                    lambda: arrived(recvc.at[pl.ds(0, 2 * nx - 1)], rc.at[0]),
+                    lambda: arrived(recvc.at[pl.ds(0, 2 * nx)], rc.at[0]),
                 )
                 for kk in range(2):
-                    slots = [base + 2 * xx + kk if step == 0 else base + xx for xx in range(nx)]
-                    cols = recvc[slots[0]]
-                    for slot in slots[1:]:
-                        cols += recvc[slot]
-                    first = 0 if step == 0 else 4 * kk
+                    cols = recvc[kk]
+                    for xx in range(1, nx):
+                        cols += recvc[2 * xx + kk]
                     for q in range(POLS):
                         at = pl.ds(LINES * q, LINES)
-                        line = jnp.broadcast_to(cols[first + q : first + q + 1], (8, LANES))
-                        send2[step, at] = send2[step, at] + jnp.where(row8 == zl * 2 + kk, line, 0.0)
+                        line = jnp.broadcast_to(cols[q : q + 1], (8, LANES))
+                        send2[0, at] = send2[0, at] + jnp.where(row8 == zl * 2 + kk, line, 0.0)
+
+            if step == 0:
+                pl.when(keeper)(add_columns)
 
             if step == 0:
                 pl.semaphore_wait(rounds.at[2], 2)
@@ -497,6 +523,22 @@
                 arrived(recvx.at[pl.ds(nx, nx - 1)], rx.at[1])
                 coupled = send3[0] - jnp.concatenate([en[y]] * POLS, axis=0) * u[0, y]
                 rest = rest - spread(alpha) * (u[1, y] + coupled) - spread(ratio_of(1)) * u[0, y]
+                many = nx * zl_count
+                either(
+                    jnp.logical_and(keeper, p == p_keep),
+                    lambda: arrived(recvd.at[pl.ds(0, many - 1)], rd.at[0]),
+                    lambda: arrived(recvd.at[pl.ds(0, many)], rd.at[0]),
+                )
+                lines = [jnp.zeros((8, LANES), F32)] * POLS
+                for t in range(zl_count):
+                    cols = recvd[t]
+                    for xx in range(1, nx):
+                        cols += recvd[xx * zl_count + t]
+                    for q in range(POLS):
+                        for kk in range(2):
+                            line = jnp.broadcast_to(cols[4 * kk + q : 4 * kk + q + 1], (8, LANES))
+                            lines[q] = jnp.where(row8 == 2 * t + kk, line, lines[q])
+                rest = rest + jnp.concatenate(lines, axis=0)
             arrived(recv2.at[pl.ds(step * nz, nz - 1)], r2.at[step])
             total = recv2[step * nz]
             for zz in range(1, nz):
@@ -542,11 +584,11 @@
                         dev((p + jp) % 2, (x + dx) % nx, z, (h + jh) % 2, kk),
                     )
 
-                for dx in (2, 1, 3, 0):
-                    for j in (3, 2, 1, 0):
-                        for kk in range(2):
-                            if (dx, j, kk) != (0, 0, 1):
-                                start(functools.partial(sums_copy, dx, j, kk))
+                targets = [(dx, j, kk) for dx in range(nx) for j in range(4) for kk in range(2)]
+                targets.sort(key=lambda t: -min(t[0], nx - t[0]) - (0, 1, 1, 2)[t[1]] - 0.6 * (t[2] == 0))
+                for target in targets:
+                    if target != (0, 0, 1):
+                        start(functools.partial(sums_copy, *target))
                 recvn[x * 4 + y] = sendn[...]
                 send3[1] = value
 
@@ -631,6 +673,7 @@
             pltpu.VMEM((rows, cols), BF),
             pltpu.VMEM((4, cols, LINES * LANES), BF),
             pltpu.VMEM((4, 8 * LINES, LANES), F32),
+            pltpu.VMEM((16, *tile), F32),
             pltpu.VMEM(dipole.shape, F32),
             pltpu.VMEM(band_energy.shape, F32),
             pltpu.SMEM(core_energy.shape, F32),
@@ -663,6 +706,7 @@
             dma((2,)), dma((1,)),
             pltpu.SemaphoreType.REGULAR, pltpu.SemaphoreType.REGULAR((3,)),
             dma((2,)), dma((2,)),
+            dma((1,)), dma((1,)),
         ],
         compiler_params=pltpu.CompilerParams(collective_id=0, has_side_effects=True),
     )(kernel_half, dipole, band_energy, core_energy, core_index)

time: 36 us -> 36 us (level)
  no operation moved by 1% of the time
where the time goes in v8:
time: 36 us; the launch traced here: 35.8 us
  Pallas kernels  35.2 us (98%)
  between operations  0.64 us (2%)
    pallas_call x1, Pallas kernels, lanczos(): pl.pallas_call(functools.partial(kernel, sizes), out_shape=(pltpu.VMEM((2...  34.5 us

profile of v8, /device:TPU:1, one launch (start us, length us, event | category | flops | bytes accessed | tf_op | source)
XLA Modules:
  0.0 35.8 jit_solution(14028297438854947898)
XLA Ops:
  0.6 34.5 %shard_map.76 = (f32[2,3]{1,0:T(2,128)S(1)}, f32[2,3]{1,0:T(2,128)S(1)}, f32[3,4096]{1,0:T(4,128)S(1)}) custom-call(bf16[4096,256]{1,0:T(8,128)(2,1)} %w_hbm.1, f32[3,4096]{1,0:T(4,128)} %dip_hbm.1, f32[2,512]{1,0:T(2,128)} %band_hbm.1, f32[4]{0:T(128)} %core_hbm.1, s32[8]{0:T(128)} %index_hbm.1), custom_call_target="tpu_custom_call" | custom-call | tf_op jit(solution)/shard_map/pallas_call | solution.py:665
  35.2 0.7 %shard_map.77 = (f32[2,3]{1,0:T(2,128)}, f32[2,3]{1,0:T(2,128)}, f32[3,4096]{1,0:T(4,128)}) custom-call(f32[2,3]{1,0:T(2,128)S(1)} %get-tuple-element.9.refs_0_, f32[2,3]{1,0:T(2,128)S(1)} %get-tuple-element.10.refs_1_, f32[3,4096]{1,0:T(4,128)S(1)} %get-tuple-element.11.refs_2_), custom_call_target="tpu_custom_call" | custom-call | tf_op jit(solution)/shard_map/pallas_call | solution.py:713

commit v9 on v7

--- a/solution.py
+++ b/solution.py
@@ -164,7 +164,9 @@
             def _():
                 left_here(recvc.at[pl.ds(0, 3)], st.at[0])
 
-            left_here(recv2.at[pl.ds(0, 2 * (nz - 1))], s2.at[0])
+            left_here(recv2.at[pl.ds(0, nz - 1)], s2.at[0])
+            left_here(recv3.at[pl.ds(0, nz - 1)], s2.at[1])
+            left_here(recv3.at[pl.ds(0, 3)], s1.at[1])
             for step in range(2):
                 left_here(recv3.at[pl.ds(0, 7)], s3.at[step])
                 left_here(recvn.at[pl.ds(0, 16 - step)], sn.at[step])
@@ -172,7 +174,7 @@
 
         either(
             owner,
-            lambda: left_here(recv1.at[pl.ds(0, 6)], s1.at[0]),
+            lambda: left_here(recv1.at[pl.ds(0, 3)], s1.at[0]),
             lambda: left_here(recv1.at[pl.ds(0, 4)], s1.at[0]),
         )
 
@@ -303,10 +305,13 @@
 
     alpha = norms = None
     for step in range(2):
-        def row_copy(j, step=step):
+        rows = ROWS if step else ROWS + 8
+
+        def row_copy(j, step=step, rows=rows):
             jh, jp = near[j]
             return send(
-                send1.at[step, j], recv1.at[y * 2 + k if step == 0 else 8 + y], s1.at[0], r1.at[step],
+                send1.at[step, j, pl.ds(0, rows)], recv1.at[y * 2 + k if step == 0 else 8 + y, pl.ds(0, rows)],
+                s1.at[step], r1.at[step],
                 member(jh, jp, 1),
             )
 
@@ -389,7 +394,6 @@
                     turn[j, 8 * t : 8 * t + 8, :] = wide[:, t * LANES : (t + 1) * LANES]
                 for q in range(POLS):
                     send1[1, j, LINES * q : LINES * (q + 1)] = turn[j, pl.ds(q, LINES, stride=8), :]
-                send1[1, j, ROWS:] = jnp.zeros((8, LANES), F32)
                 if j:
                     start(functools.partial(row_copy, j))
             arrived(recvx.at[pl.ds(0, nx - 1)], rx.at[0])
@@ -444,7 +448,7 @@
                 chip_copy(1).start()
 
         @pl.when(owner)
-        def _(step=step, own_sums=own_sums):
+        def _(step=step, own_sums=own_sums, rows=rows):
             if step == 0:
                 pl.semaphore_wait(rounds.at[1], 2)
                 above_and_below(rounds.at[2])
@@ -452,13 +456,14 @@
                 sendx[1] = own_sums
                 share(1, 1)
                 share(1, 0)
-            recv1[y * 2 + k if step == 0 else 8 + y] = send1[step, 0]
+            part = pl.ds(0, rows)
+            recv1[y * 2 + k if step == 0 else 8 + y, part] = send1[step, 0, part]
             members = 4 if step else 8
-            arrived(recv1.at[pl.ds(step * 8, members - 1)], r1.at[step])
-            total = recv1[step * 8]
+            arrived(recv1.at[pl.ds(step * 8, members - 1), part], r1.at[step])
+            total = recv1[step * 8, part]
             for g in range(1, members):
-                total += recv1[step * 8 + g]
-            send2[step] = total
+                total += recv1[step * 8 + g, part]
+            send2[step, part] = total
 
             @pl.when(keeper)
             def _():
@@ -483,13 +488,13 @@
                 pl.semaphore_wait(rounds.at[2], 2)
             def z_copy(d):
                 return send(
-                    send2.at[step], recv2.at[step * nz + z], s2.at[0], r2.at[step],
+                    send2.at[step, part], recv2.at[step * nz + z, part], s2.at[step], r2.at[step],
                     dev(p, x, (z + d) % nz, h, 1),
                 )
 
             for d in far_first:
                 start(functools.partial(z_copy, d))
-            recv2[step * nz + z] = send2[step]
+            recv2[step * nz + z, part] = send2[step, part]
             rest = jnp.concatenate([en[y]] * POLS, axis=0) * u[step, y]
             if step == 0:
                 transpose()
@@ -497,10 +502,10 @@
                 arrived(recvx.at[pl.ds(nx, nx - 1)], rx.at[1])
                 coupled = send3[0] - jnp.concatenate([en[y]] * POLS, axis=0) * u[0, y]
                 rest = rest - spread(alpha) * (u[1, y] + coupled) - spread(ratio_of(1)) * u[0, y]
-            arrived(recv2.at[pl.ds(step * nz, nz - 1)], r2.at[step])
-            total = recv2[step * nz]
+            arrived(recv2.at[pl.ds(step * nz, nz - 1), part], r2.at[step])
+            total = recv2[step * nz, part]
             for zz in range(1, nz):
-                total += recv2[step * nz + zz]
+                total += recv2[step * nz + zz, part]
             value = total[:ROWS] + rest
 
             def chunk_copy(j, kk):
@@ -654,9 +659,9 @@
             pltpu.VMEM((nx * 4, *tile), F32),
             dma((3,)), dma((2,)),
             dma((1,)), dma((1,)),
+            dma((2,)), dma((2,)),
             dma((1,)), dma((2,)),
-            dma((1,)), dma((2,)),
-            dma((1,)), dma((2,)),
+            dma((2,)), dma((2,)),
             dma((2,)), dma((8,)),
             dma((1,)), dma((1,)),
             dma((1,)), dma((2,)),

time: 36 us -> 36 us (level)
  no operation moved by 1% of the time
where the time goes in v9:
time: 36 us; the launch traced here: 35.8 us
  Pallas kernels  35.2 us (98%)
  between operations  0.64 us (2%)
    pallas_call x1, Pallas kernels, lanczos(): pl.pallas_call(functools.partial(kernel, sizes), out_shape=(pltpu.VMEM((2...  34.5 us

profile of v9, /device:TPU:1, one launch (start us, length us, event | category | flops | bytes accessed | tf_op | source)
XLA Modules:
  0.0 35.8 jit_solution(15850328416520249855)
XLA Ops:
  0.6 34.5 %shard_map.76 = (f32[2,3]{1,0:T(2,128)S(1)}, f32[2,3]{1,0:T(2,128)S(1)}, f32[3,4096]{1,0:T(4,128)S(1)}) custom-call(bf16[4096,256]{1,0:T(8,128)(2,1)} %w_hbm.1, f32[3,4096]{1,0:T(4,128)} %dip_hbm.1, f32[2,512]{1,0:T(2,128)} %band_hbm.1, f32[4]{0:T(128)} %core_hbm.1, s32[8]{0:T(128)} %index_hbm.1), custom_call_target="tpu_custom_call" | custom-call | tf_op jit(solution)/shard_map/pallas_call | solution.py:628
  35.2 0.7 %shard_map.77 = (f32[2,3]{1,0:T(2,128)}, f32[2,3]{1,0:T(2,128)}, f32[3,4096]{1,0:T(4,128)}) custom-call(f32[2,3]{1,0:T(2,128)S(1)} %get-tuple-element.9.refs_0_, f32[2,3]{1,0:T(2,128)S(1)} %get-tuple-element.10.refs_1_, f32[3,4096]{1,0:T(4,128)S(1)} %get-tuple-element.11.refs_2_), custom_call_target="tpu_custom_call" | custom-call | tf_op jit(solution)/shard_map/pallas_call | solution.py:674
